TPU v7x, 128 devices: a whole 4x4x4 slice. The times are simulated.
128 devices in a mesh: row: 16 (over z, x), col: 8 (over y, core).
Axes of the slice: x: 4, y: 4, z: 4, core: 2. Of those that a mesh axis runs over, the one named last changes fastest.
Arguments:
- cam_jac: float32 [512, 18, 512], P(('row', 'col')), may hold values from -1 to 1
- land_jac: float32 [512, 6, 512], P(('row', 'col')), may hold values from -5 to 5
- resid: float32 [512, 2, 512], P(('row', 'col')), may hold values from -20 to 20
- obs_cam: int32 [512, 512], P(('row', 'col')), may hold values from 0 to 127
- obs_land: int32 [512, 512], P(('row', 'col')), may hold values from 0 to 127
- pairs: int32 [512, 2], P(('row', 'col')), may hold values from 0 to 31, as said below
- cam_damp: float32 [18432], P(('row', 'col')), may hold values from 1 to 10
Outputs:
- cam_step: float32 [18432], P(('row', 'col'))
- land_step: float32 [512, 3, 128], P(('row', 'col'))
Inputs may be any that keep to these rules, and one draw needn't show every extreme that they name: `pairs`: clusters are laid out device by device, 4 a device, devices in order of row, then col. A cluster held at grid row r and grid column c is seen by a first group in [r * 2, (r + 1) * 2) and a different second group in [c * 4, (c + 1) * 4).
All inputs are finite; a program needn't handle non-finite values.
Results may differ from a plain program's by a relative error of at most 0.0003.
Values sent between devices are 32-bit elements; how exact they have to be, the bound alone decides.
A program may use at most 384 MiB of HBM per device.

v0:
```python
import jax
import jax.numpy as jnp
from jax import lax
from jax.sharding import PartitionSpec as P

G = 32
CAM = 64
LM = 128
ITERS = 2


DAMPING = 1.0
HIGHEST = lax.Precision.HIGHEST


def cholesky_three(normal):
    root_first = jnp.sqrt(normal[0])
    inv_first = 1.0 / root_first
    low_one = normal[1] * inv_first
    low_two = normal[2] * inv_first
    inv_second = 1.0 / jnp.sqrt(normal[4] - low_one * low_one)
    low_three = (normal[5] - low_two * low_one) * inv_second
    inv_third = 1.0 / jnp.sqrt(normal[8] - low_two * low_two - low_three * low_three)
    return jnp.stack([inv_first, low_one, low_two, inv_second, low_three, inv_third])


def lower_solve(factor, first, second, third):
    out_one = first * factor[0]
    out_two = (second - factor[1] * out_one) * factor[3]
    out_three = (third - factor[2] * out_one - factor[4] * out_two) * factor[5]
    return jnp.stack([out_one, out_two, out_three])


def upper_solve(factor, first, second, third):
    out_three = third * factor[5]
    out_two = (second - factor[4] * out_three) * factor[3]
    out_one = (first - factor[1] * out_two - factor[2] * out_three) * factor[0]
    return jnp.stack([out_one, out_two, out_three])


def cluster_schur(cam_jac, land_jac, resid, obs_cam, obs_land):
    count = obs_cam.shape[0]
    width = CAM * 9
    cam_rows = cam_jac.reshape(2, 9, count)
    land_rows = land_jac.reshape(2, 3, count)
    coupled = (
        cam_rows[0][:, None, :] * land_rows[0][None] + cam_rows[1][:, None, :] * land_rows[1][None]
    )
    land_outer = (
        land_rows[0][:, None, :] * land_rows[0][None]
        + land_rows[1][:, None, :] * land_rows[1][None]
    ).reshape(9, count)
    cam_outer = (
        cam_rows[0][:, None, :] * cam_rows[0][None] + cam_rows[1][:, None, :] * cam_rows[1][None]
    ).reshape(81, count)
    cam_grad = cam_rows[0] * resid[0] + cam_rows[1] * resid[1]
    land_grad = land_rows[0] * resid[0] + land_rows[1] * resid[1]
    land_onehot = (obs_land[None, :] == jnp.arange(LM, dtype=jnp.int32)[:, None]).astype(
        jnp.float32
    )
    cam_onehot = (obs_cam[None, :] == jnp.arange(2 * CAM, dtype=jnp.int32)[:, None]).astype(
        jnp.float32
    )
    land_normal = jnp.dot(land_outer, land_onehot.T, precision=HIGHEST) + DAMPING * jnp.eye(
        3, dtype=jnp.float32
    ).reshape(9, 1)
    land_total = jnp.dot(land_grad, land_onehot.T, precision=HIGHEST)
    cam_normal = jnp.dot(cam_outer, cam_onehot.T, precision=HIGHEST)
    cam_total = jnp.dot(cam_grad, cam_onehot.T, precision=HIGHEST)
    factor = cholesky_three(land_normal)
    obs_factor = jnp.dot(factor, land_onehot, precision=HIGHEST)
    solved = jnp.stack(
        [
            lower_solve(obs_factor, coupled[param, 0], coupled[param, 1], coupled[param, 2])
            for param in range(9)
        ]
    )
    spread = solved.reshape(27, 1, count) * land_onehot[None]
    placed = jnp.einsum("co,xlo->cxl", cam_onehot, spread, precision=HIGHEST)
    coupling = placed.reshape(2 * width, 3 * LM)
    tvector = lower_solve(factor, land_total[0], land_total[1], land_total[2]).reshape(3 * LM)
    blocks = cam_normal.T.reshape(2, CAM, 9, 9)
    eye_cam = jnp.eye(CAM, dtype=jnp.float32)
    upper_first = (eye_cam[:, None, :, None] * blocks[0][:, :, None, :]).reshape(width, width)
    upper_second = (eye_cam[:, None, :, None] * blocks[1][:, :, None, :]).reshape(width, width)
    coupling_first = coupling[:width]
    coupling_second = coupling[width:]
    diag_first = upper_first - jnp.dot(coupling_first, coupling_first.T, precision=HIGHEST)
    cross = -jnp.dot(coupling_first, coupling_second.T, precision=HIGHEST)
    diag_second = upper_second - jnp.dot(coupling_second, coupling_second.T, precision=HIGHEST)
    right = -cam_total.T.reshape(2 * width) + jnp.dot(coupling, tvector, precision=HIGHEST)
    return (diag_first, cross, diag_second, right[:width], right[width:], coupling, tvector, factor)


def add_block(target, block, row_start, col_start):
    current = lax.dynamic_slice(target, (row_start, col_start), block.shape)
    return lax.dynamic_update_slice(target, current + block, (row_start, col_start))


def add_segment(target, piece, start):
    current = lax.dynamic_slice_in_dim(target, start, piece.shape[0], 0)
    return lax.dynamic_update_slice_in_dim(target, current + piece, start, 0)


def whole_vector(shard_vector):
    whole = lax.all_gather(shard_vector, ("row", "col"), axis=0, tiled=True)
    return whole


def residual_weight(residual, precon_res):
    return lax.psum(jnp.sum(residual * precon_res), ("row", "col"))


def per_device(cam_jac, land_jac, resid, obs_cam, obs_land, pairs, cam_damp):
    n_row = lax.axis_size("row")
    n_col = lax.axis_size("col")
    row_pos = lax.axis_index("row")
    col_pos = lax.axis_index("col")
    width = CAM * 9
    total = G * width
    rows_seg = total // n_row
    cols_seg = total // n_col
    shard = total // (n_row * n_col)
    grid = jnp.zeros((rows_seg, cols_seg), jnp.float32)
    row_stack = jnp.zeros((rows_seg, width), jnp.float32)
    row_right = jnp.zeros((rows_seg,), jnp.float32)
    col_stack = jnp.zeros((cols_seg, width), jnp.float32)
    col_right = jnp.zeros((cols_seg,), jnp.float32)
    kept = []
    for local in range(cam_jac.shape[0]):
        diag_first, cross, diag_second, right_first, right_second, coupling, tvector, factor = (
            cluster_schur(
                cam_jac[local], land_jac[local], resid[local], obs_cam[local], obs_land[local]
            )
        )
        first = pairs[local, 0]
        second = pairs[local, 1]
        row_start = first * width - row_pos * rows_seg
        col_start = second * width - col_pos * cols_seg
        grid = add_block(grid, cross, row_start, col_start)
        row_stack = add_block(row_stack, diag_first, row_start, 0)
        row_right = add_segment(row_right, right_first, row_start)
        col_stack = add_block(col_stack, diag_second, col_start, 0)
        col_right = add_segment(col_right, right_second, col_start)
        kept.append((coupling, tvector, factor, first, second))
    col_sum, col_right = lax.psum((col_stack, col_right), "row")
    offset = row_pos * rows_seg - col_pos * cols_seg
    on_diag = ((offset >= 0) & (offset + rows_seg <= cols_seg)).astype(jnp.float32)
    start = jnp.clip(offset, 0, cols_seg - rows_seg)
    row_stack = row_stack + on_diag * lax.dynamic_slice_in_dim(col_sum, start, rows_seg, 0)
    row_right = row_right + on_diag * lax.dynamic_slice_in_dim(col_right, start, rows_seg, 0)
    my_rows, my_right = (
        lax.psum_scatter(row_stack, "col", scatter_dimension=0, tiled=True),
        lax.psum_scatter(row_right, "col", scatter_dimension=0, tiled=True),
    )
    first_index = row_pos * rows_seg + col_pos * shard
    group_start = first_index // width * width
    inner = first_index - group_start
    diag_values = jnp.diagonal(lax.dynamic_slice_in_dim(my_rows, inner, shard, 1))
    precond = 1.0 / (diag_values + cam_damp)
    solution = jnp.zeros((shard,), jnp.float32)
    residual = my_right
    precon_res = precond * residual
    direction = precon_res
    norm_now = residual_weight(residual, precon_res)
    for step in range(ITERS):
        whole = whole_vector(direction)
        col_part = lax.dynamic_slice_in_dim(whole, col_pos * cols_seg, cols_seg)
        row_part = lax.dynamic_slice_in_dim(whole, row_pos * rows_seg, rows_seg)
        group_part = lax.dynamic_slice_in_dim(whole, group_start, width)
        forward = jnp.dot(grid, col_part, precision=HIGHEST)
        backward = jnp.dot(row_part, grid, precision=HIGHEST)
        partial_sum = jnp.zeros((total,), jnp.float32)
        partial_sum = add_segment(partial_sum, forward, row_pos * rows_seg)
        partial_sum = add_segment(partial_sum, backward, col_pos * cols_seg)
        image = lax.psum_scatter(partial_sum, ("row", "col"), scatter_dimension=0, tiled=True)
        image = image + jnp.dot(my_rows, group_part, precision=HIGHEST) + cam_damp * direction
        alpha = norm_now / lax.psum(jnp.sum(direction * image), ("row", "col"))
        solution = solution + alpha * direction
        residual = residual - alpha * image
        if step + 1 < ITERS:
            precon_res = precond * residual
            norm_next = residual_weight(residual, precon_res)
            direction = precon_res + norm_next / norm_now * direction
            norm_now = norm_next
    whole_solution = whole_vector(solution)
    steps_out = []
    for coupling, tvector, factor, first, second in kept:
        first_part = lax.dynamic_slice_in_dim(whole_solution, first * width, width)
        second_part = lax.dynamic_slice_in_dim(whole_solution, second * width, width)
        camera_part = jnp.concatenate([first_part, second_part])
        summed = (tvector + jnp.dot(camera_part, coupling, precision=HIGHEST)).reshape(3, LM)
        steps_out.append(-upper_solve(factor, summed[0], summed[1], summed[2]))
    return (solution, jnp.stack(steps_out))


def solution(mesh):
    in_specs = (
        P(("row", "col"), None, None),
        P(("row", "col"), None, None),
        P(("row", "col"), None, None),
        P(("row", "col"), None),
        P(("row", "col"), None),
        P(("row", "col"), None),
        P(("row", "col")),
    )
    out_specs = (P(("row", "col")), P(("row", "col"), None, None))
    return jax.shard_map(
        per_device, mesh=mesh, in_specs=in_specs, out_specs=out_specs, check_vma=False
    )
```

profile of v0, /device:TPU:1, one launch (start us, length us, event | category | flops | bytes accessed | tf_op | source)
XLA Modules:
  0.0 1562.2 jit_solution(15703655608987239148)
XLA Ops:
  36.8 5.1 fusion.6
  43.7 4.7 fusion.4
  63.3 51.1 %broadcast_multiply_fusion = (f32[64,9,64,9]{3,2,1,0:T(8,128)}, f32[64,9,64,9]{3,2,1,0:T(8,128)}, f32[64,9,64,9]{3,2,1,0:T(8,128)}, f32[64,9,64,9]{3,2,1,0:T(8,1...) fusion(f32[64,9,9]{2,1,0:T(8,128)S(1)} %copy.112, ...), kind=kLoop, calls=%fused_computation.1 | loop fusion | flops 2654208 | bytes 10799104 | tf_op jit(solution)/shard_map/mul | solution.py:85
  114.4 14.0 mul.2804
  133.0 15.0 mul.2808
  160.5 8.8 dynamic_update_slice.84
  169.3 5.4 subtract_add_fusion.2
  174.7 8.4 dynamic_update_slice.85
  183.1 14.7 mul.2812
  200.5 5.9 subtract_add_fusion.1
  206.4 9.3 dynamic_update_slice.86
  215.7 14.7 mul.2816
  233.1 5.7 subtract_add_fusion
  238.8 9.3 dynamic_update_slice.87
  250.8 15.7 %mul.2769 = f32[576,576]{1,0:T(8,128)} reshape(f32[64,9,64,9]{3,2,1,0:T(8,128)} %get-tuple-element.262) | data formatting | bytes 2654208 | tf_op jit(solution)/shard_map/mul | solution.py:84
  269.2 15.2 mul.2779
  294.5 11.8 dynamic_update_slice.80
  306.3 5.3 subtract_add_fusion.5
  311.6 12.3 dynamic_update_slice.81
  324.0 14.9 mul.2789
  345.1 5.7 subtract_add_fusion.4
  350.7 12.3 dynamic_update_slice.82
  363.1 14.7 mul.2799
  383.8 5.6 subtract_add_fusion.3
  389.4 12.1 dynamic_update_slice.83
  444.7 5.3 convolution_negate_fusion
  450.1 4.7 broadcast_in_dim.16
  454.7 8.6 dynamic_update_slice.88
  463.4 5.9 negate_add_fusion.2
  469.3 8.7 dynamic_update_slice.89
  478.0 5.9 negate_add_fusion.1
  483.9 9.4 dynamic_update_slice.90
  508.8 60.2 %psum.42 = f32[2304]{0:T(1024)} all-reduce(f32[2304]{0:T(1024)S(1)} %get-tuple-element.271), channel_id=1, replica_groups=mesh['row'=16,'col'=8] {'row'}, use_global_device_ids=true, to_apply=%region_0.0 | all-reduce | flops 2304 | bytes 18432 | tf_op jit(solution)/shard_map/psum | solution.py:146
  569.7 28.2 %all-reduce.3 = f32[1152]{0:T(1024)} all-reduce(f32[1152]{0:T(1024)S(1)} %multiply_add_fusion.13), channel_id=2, replica_groups=mesh['row'=16,'col'=8] {'col'}, use_global_device_ids=true, to_apply=%region_1.0.clone | all-reduce | flops 1152 | bytes 9216
  607.0 6.0 negate_add_fusion
  613.0 9.5 dynamic_update_slice.91
  622.5 118.3 %all-reduce.16.cloned.1.call-done = f32[18432]{0:T(1024)} async-done(((f32[18432]{0:T(1024)}), f32[18432]{0:T(1024)}) %all-reduce.16.cloned.1.call-update) | async-done | bytes 73744
  743.7 11.9 convolution_reduce_fusion.3
  755.7 5.0 convolution_reduce_fusion.1
  765.8 135.9 %all-reduce.22.cloned.1.call-done = f32[18432]{0:T(1024)} async-done(((f32[18432]{0:T(1024)}), f32[18432]{0:T(1024)}) %all-reduce.22.cloned.1.call-update) | async-done | bytes 73744
  903.2 63.4 %all-reduce.6 = (f32[]{:T(128)}, f32[]{:T(128)}) all-reduce(f32[]{:T(128)} %get-tuple-element.9, f32[]{:T(128)} %get-tuple-element.8), channel_id=1, replica_groups=mesh['row'=16,'col'=8] {'row','col'}, use_global_device_ids=true, to_apply=%region_5.6 | all-reduce | flops 2 | bytes 16 | tf_op jit(solution)/shard_map/psum | solution.py:111
  969.4 63.2 %psum.46 = f32[]{:T(128)} all-reduce(f32[]{:T(128)} %multiply_reduce_fusion), channel_id=1, replica_groups=mesh['row'=16,'col'=8] {'row','col'}, use_global_device_ids=true, to_apply=%region_10.11 | all-reduce | flops 1 | bytes 8 | tf_op jit(solution)/shard_map/psum | solution.py:111
  1036.3 136.8 %all-reduce.18.cloned.1.call-done = f32[18432]{0:T(1024)} async-done(((f32[18432]{0:T(1024)}), f32[18432]{0:T(1024)}) %all-reduce.18.cloned.1.call-update) | async-done | bytes 73744
  1175.2 11.8 convolution_reduce_fusion.2
  1187.8 9.0 convolution_reduce_fusion
  1201.9 135.8 %all-reduce.24.cloned.1.call-done = f32[18432]{0:T(1024)} async-done(((f32[18432]{0:T(1024)}), f32[18432]{0:T(1024)}) %all-reduce.24.cloned.1.call-update) | async-done | bytes 73744
  1339.2 63.2 %psum.47 = f32[]{:T(128)} all-reduce(f32[]{:T(128)} %fusion.331), channel_id=1, replica_groups=mesh['row'=16,'col'=8] {'row','col'}, use_global_device_ids=true, to_apply=%region_13.14 | all-reduce | flops 1 | bytes 8 | tf_op jit(solution)/shard_map/psum | solution.py:178
  1405.8 137.4 %all-reduce.20.cloned.1.call-done = f32[18432]{0:T(1024)} async-done(((f32[18432]{0:T(1024)}), f32[18432]{0:T(1024)}) %all-reduce.20.cloned.1.call-update) | async-done | bytes 73744
  (529 shorter events, 193.7 us)
Async XLA Ops:
  7.2 394.4 %all-reduce.14.cloned.1.call-start = ((), (), s32[]{:S(2)}) async-start(), calls=%async_computation.1 | async-start | bytes 10616832 | tf_op jit(solution)/shard_map/psum | solution.py:146
  8.0 5.2 copy-start.105
  8.1 9.4 copy-start.103
  8.1 12.4 copy-start.101
  8.1 12.4 copy-start.102
  8.1 13.4 copy-start.107
  8.1 15.7 %copy-start.99 = (f32[1,1,512]{2,1,0:T(1,128)}, f32[1,1,512]{2,1,0:T(1,128)S(1)}, u32[]{:S(2)}) copy-start(f32[1,1,512]{2,1,0:T(1,128)S(1)} %get-tuple-element.263) | copy-start | bytes 6148
  8.1 15.7 %copy-start.100 = (f32[1,1,512]{2,1,0:T(1,128)}, f32[1,1,512]{2,1,0:T(1,128)S(1)}, u32[]{:S(2)}) copy-start(f32[1,1,512]{2,1,0:T(1,128)S(1)} %get-tuple-element.270) | copy-start | bytes 6148
  9.4 12.6 copy-start.35
  9.4 12.6 copy-start.36
  9.4 12.6 copy-start.37
  9.4 12.6 copy-start.39
  9.5 12.6 copy-start.41
  9.5 12.6 copy-start.43
  9.5 15.4 copy-start.33
  9.5 15.4 copy-start.34
  12.0 8.1 copy-start.109
  18.3 7.0 copy-start.70
  18.3 7.0 copy-start.72
  18.3 7.8 copy-start.68
  18.3 7.8 copy-start.74
  18.3 7.8 copy-start.76
  20.2 6.1 copy-start.54
  26.3 23.5 %copy-start.53 = (s32[1,512]{1,0:T(1,128)}, s32[1,512]{1,0:T(1,128)S(1)}, u32[]{:S(2)}) copy-start(s32[1,512]{1,0:T(1,128)S(1)} %get-tuple-element.287) | copy-start | bytes 6148
  26.3 29.6 %copy-start.52 = (s32[1,512]{1,0:T(1,128)}, s32[1,512]{1,0:T(1,128)S(1)}, u32[]{:S(2)}) copy-start(s32[1,512]{1,0:T(1,128)S(1)} %get-tuple-element.284) | copy-start | bytes 6148
  132.9 21.1 %copy-start.5 = (f32[576,384]{1,0:T(8,128)}, f32[576,384]{1,0:T(8,128)S(1)}, u32[]{:S(2)}) copy-start(f32[576,384]{1,0:T(8,128)S(1)} %slice.1314) | copy-start | bytes 2654212
  154.0 15.3 copy-start.6
  160.5 8.8 copy-start.20
  200.5 5.9 copy-start.7
  233.1 5.8 copy-start.4
  248.2 349.8 %reduce-scatter.4.cloned.1.call-start = ((), (), s32[]{:S(2)}) async-start(), calls=%async_computation.5 | async-start | bytes 3317760
  269.2 21.2 %copy-start.9 = (f32[576,384]{1,0:T(8,128)}, f32[576,384]{1,0:T(8,128)S(1)}, u32[]{:S(2)}) copy-start(f32[576,384]{1,0:T(8,128)S(1)} %slice.1302) | copy-start | bytes 2654212
  290.4 15.9 %copy-start.10 = (f32[576,384]{1,0:T(8,128)}, f32[576,384]{1,0:T(8,128)S(1)}, u32[]{:S(2)}) copy-start(f32[576,384]{1,0:T(8,128)S(1)} %slice.1305) | copy-start | bytes 2654212
  345.0 5.7 copy-start.11
  383.8 5.6 copy-start.8
  409.2 331.6 %all-reduce.16.cloned.1.call-start = ((), (), s32[]{:S(2)}) async-start(), calls=%async_computation.2 | async-start | bytes 147456
  493.3 5.3 copy-start.1
  493.3 5.3 copy-start.56
  500.9 104.4 %copy-start.50 = (f32[144]{0:T(256)S(1)}, f32[144]{0:T(256)}, u32[]{:S(2)}) copy-start(f32[144]{0:T(256)} %param.13) | copy-start | bytes 1732
  604.6 8.4 copy-start.51
  606.7 295.0 %all-reduce.22.cloned.1.call-start = ((), (), s32[]{:S(2)}) async-start(), calls=%async_computation.6 | async-start | bytes 147456
  743.7 11.9 copy-start
  764.3 408.7 %all-reduce.18.cloned.1.call-start = ((), (), s32[]{:S(2)}) async-start(), calls=%async_computation.3 | async-start | bytes 147456
  1036.2 301.6 %all-reduce.24.cloned.1.call-start = ((), (), s32[]{:S(2)}) async-start(), calls=%async_computation.7 | async-start | bytes 147456
  1200.5 342.8 %all-reduce.20.cloned.1.call-start = ((), (), s32[]{:S(2)}) async-start(), calls=%async_computation.4 | async-start | bytes 147456
  1543.2 5.1 copy-start.2
  1544.4 5.1 copy-start.79
  1544.4 5.1 copy-start.81
  (73 other events, 182.2 us)
Sparse Core Ops, SparseCore 0:
  248.3 116.9 all-reduce.13
  409.3 36.3 reduce-scatter.3
  606.8 133.9 all-reduce.15
  764.5 137.2 all-reduce.21
  1036.3 136.6 all-reduce.17
  1200.6 137.1 all-reduce.23
  1405.9 137.2 all-reduce.19
where the time goes:
time: 1580 us; the launch traced here: 1560 us
  waiting for transfers between devices  664 us (42%)
  local copies, waits for them, and re-layouts  363 us (23%)
  blocking collectives  278 us (18%)
  matrix products  143 us (9%)
  other arithmetic  87 us (6%)
  between operations  26.5 us (2%)
    unnamed x13, waiting for transfers between devices  664 us
    psum x2, blocking collectives, residual_weight(): return lax.psum(jnp.sum(residual * precon_res), ('row', 'col'))  127 us
    dynamic_update_slice x12, local copies, waits for them, and re-layouts, add_block(): lax.dynamic_update_slice(target, current + block, (row_start, col_start))  121 us
    mul x16, local copies, waits for them, and re-layouts, cluster_schur(): eye_cam[:, None, :, None] * blocks[0][:, :, None, :]  74.6 us
    mul x16, local copies, waits for them, and re-layouts, cluster_schur(): eye_cam[:, None, :, None] * blocks[1][:, :, None, :]  67.8 us
    psum x1, blocking collectives, per_device(): alpha = norm_now / lax.psum(jnp.sum(direction * image), ('row', 'col'))  63.2 us
    psum x1, blocking collectives, per_device(): col_sum, col_right = lax.psum((col_stack, col_right), 'row')  60.2 us
    mul x1, other arithmetic, cluster_schur(): eye_cam[:, None, :, None] * blocks[1][:, :, None, :]  51.1 us
  transfers between devices with their start and end apart: 7, of which 5 were waited for; matrix products, arithmetic and copies ran while one was open for 17% of the time, Pallas kernels for 0%

commit v1 on v0

v1 whole, which is shorter than its diff:
```python
import jax
import jax.numpy as jnp
from jax import lax
from jax.experimental import pallas as pl
from jax.experimental.pallas import tpu as pltpu
from jax.sharding import PartitionSpec as P

DAMPING = 1.0
MESH = pl.DeviceIdType.MESH
LANES = 128


def lane_gather(table, index):
    rows = table.shape[0]
    dims = lax.GatherDimensionNumbers(
        offset_dims=(),
        collapsed_slice_dims=(1,),
        start_index_map=(1,),
        operand_batching_dims=(0,),
        start_indices_batching_dims=(0,),
    )
    pieces = []
    for at in range(0, index.shape[1], LANES):
        piece = jnp.broadcast_to(index[:, at : at + LANES], (rows, LANES))
        pieces.append(
            lax.gather(
                table,
                piece[..., None],
                dims,
                slice_sizes=(1, 1),
                mode=lax.GatherScatterMode.PROMISE_IN_BOUNDS,
            )
        )
    return pieces[0] if len(pieces) == 1 else jnp.concatenate(pieces, axis=1)


def exact_dot(x, onehot):
    rows = x.shape[0]
    high = x.astype(jnp.bfloat16)
    rest = x - high.astype(jnp.float32)
    mid = rest.astype(jnp.bfloat16)
    low = (rest - mid.astype(jnp.float32)).astype(jnp.bfloat16)
    stacked = jnp.concatenate([high, mid, low], axis=0)
    out = jnp.dot(stacked, onehot, preferred_element_type=jnp.float32)
    return out[:rows] + (out[rows : 2 * rows] + out[2 * rows :])


def rows_of(pieces, rows):
    have = sum(p.shape[0] for p in pieces)
    if have < rows:
        pieces = list(pieces) + [jnp.zeros((rows - have, pieces[0].shape[1]), jnp.float32)]
    return jnp.concatenate(pieces, axis=0)


def col_sum(x):
    return jnp.sum(x, axis=0, keepdims=True)


def lower_solve(f, a, b, c):
    one = a * f[0]
    two = (b - f[1] * one) * f[3]
    three = (c - f[2] * one - f[4] * two) * f[5]
    return one, two, three


def upper_solve(f, a, b, c):
    three = c * f[5]
    two = (b - f[4] * three) * f[3]
    one = (a - f[1] * two - f[2] * three) * f[0]
    return one, two, three


def normal_solve(f, a, b, c):
    return upper_solve(f, *lower_solve(f, a, b, c))


def cholesky_three(v):
    inv_first = 1.0 / jnp.sqrt(v[0])
    low_one = v[1] * inv_first
    low_two = v[2] * inv_first
    inv_second = 1.0 / jnp.sqrt(v[3] - low_one * low_one)
    low_three = (v[4] - low_two * low_one) * inv_second
    inv_third = 1.0 / jnp.sqrt(v[5] - low_two * low_two - low_three * low_three)
    return inv_first, low_one, low_two, inv_second, low_three, inv_third


def make_kernel(n_row, n_col, n_cl, n_obs):
    f32 = jnp.float32

    def kernel(
        pairs_ref, cj_ref, lj_ref, re_ref, oc_ref, ol_ref, damp_ref,
        cam_ref, land_ref,
        jac, one_cam, one_land, fac, yvec, msg1, msg2, sums,
        in1, in2, zbuf, tbuf, sc1, sc2, stot,
        s1, r1, s2, r2, s3, r3, s4, r4, s5, r5, s6, r6,
    ):
        row = lax.axis_index("row")
        col = lax.axis_index("col")
        hub_col = row // 2
        is_hub = col == hub_col
        up = lambda i: lax.rem(row + i, n_row)
        over = lambda i: lax.rem(col + i, n_col)

        barrier = pltpu.get_barrier_semaphore()
        for i in range(1, n_row):
            pl.semaphore_signal(barrier, inc=1, device_id=(up(i), col), device_id_type=MESH)
        for i in range(1, n_col):
            pl.semaphore_signal(barrier, inc=1, device_id=(row, over(i)), device_id_type=MESH)

        lane = lax.broadcasted_iota(jnp.int32, (16, LANES), 1)
        sub = lax.broadcasted_iota(jnp.int32, (16, LANES), 0)
        left = lane < 64

        flat = (lane - 16 * col) * 9 + sub
        mine = (lane >= 16 * col) & (lane < 16 * col + 16) & (sub < 9)
        flat = jnp.where(mine, flat, 0)
        damp_low = jnp.broadcast_to(damp_ref[:, :LANES], (16, LANES))
        damp_high = jnp.broadcast_to(
            jnp.concatenate([damp_ref[:, LANES:], jnp.zeros((1, 2 * LANES - 144), f32)], axis=1),
            (16, LANES),
        )

        def gather_rows(table, index):
            dims = lax.GatherDimensionNumbers((), (1,), (1,), (0,), (0,))
            return lax.gather(
                table, index[..., None], dims, slice_sizes=(1, 1),
                mode=lax.GatherScatterMode.PROMISE_IN_BOUNDS,
            )

        damp = jnp.where(
            flat < LANES,
            gather_rows(damp_low, jnp.minimum(flat, LANES - 1)),
            gather_rows(damp_high, jnp.maximum(flat - LANES, 0)),
        )
        damp = jnp.where(mine, damp, 0.0)

        first = [pairs_ref[k, 0] - 2 * row for k in range(n_cl)]
        second = [pairs_ref[k, 1] - 4 * col for k in range(n_cl)]

        def place(tiles, out, k):
            rolled = pltpu.roll(out, 64, axis=1)
            half = lax.broadcasted_iota(jnp.int32, out.shape, 1) < 64

            def pick(cond, x):
                return jnp.where(cond, x, 0.0)

            a, b = first[k], second[k]
            return (
                tiles[0] + jnp.where(half, pick(a == 0, out), pick(a == 1, rolled)),
                tiles[1] + jnp.where(half, pick(b == 0, rolled), pick(b == 1, out)),
                tiles[2] + jnp.where(half, pick(b == 2, rolled), pick(b == 3, out)),
            )

        def vector_of(tiles, k):
            a, b = first[k], second[k]
            own = jnp.where(a == 0, tiles[0], pltpu.roll(tiles[0], 64, axis=1))
            other = jnp.where(b < 2, tiles[1], tiles[2])
            other = jnp.where((b == 1) | (b == 3), other, pltpu.roll(other, 64, axis=1))
            return jnp.where(left, own, other)

        keys = oc_ref[...] * LANES + ol_ref[...]
        keys_f = jnp.concatenate([keys.astype(f32), jnp.zeros((8 - n_cl, n_obs), f32)], axis=0)
        keys_t = keys_f.T
        cam_iota = lax.broadcasted_iota(jnp.int32, (LANES, n_obs), 0)
        zero = jnp.zeros((32, LANES), f32)
        tiles = (zero, zero, zero)
        for k in range(n_cl):
            cams = oc_ref[k : k + 1, :]
            lands = ol_ref[k : k + 1, :]
            jac[k, 0] = rows_of([cj_ref[k, 0:9, :]], 16)
            jac[k, 1] = rows_of([cj_ref[k, 9:18, :]], 16)
            one_cam[k] = jnp.where(cam_iota == cams, 1.0, 0.0).astype(jnp.bfloat16).T
            one_land[k] = jnp.where(cam_iota == lands, 1.0, 0.0).astype(jnp.bfloat16).T
            match = jnp.where(keys_t[:, k : k + 1] == keys_f[k : k + 1, :], 1.0, 0.0).astype(
                jnp.bfloat16
            )
            j0, j1 = jac[k, 0], jac[k, 1]
            ka = [lj_ref[k, b : b + 1, :] for b in range(3)]
            kb = [lj_ref[k, 3 + b : 4 + b, :] for b in range(3)]
            e0, e1 = re_ref[k, 0:1, :], re_ref[k, 1:2, :]
            stats = [
                ka[i] * ka[j] + kb[i] * kb[j]
                for i, j in ((0, 0), (0, 1), (0, 2), (1, 1), (1, 2), (2, 2))
            ] + [ka[b] * e0 + kb[b] * e1 for b in range(3)]
            total = exact_dot(rows_of(stats, 16), one_land[k])
            v = [total[i : i + 1] for i in range(9)]
            v[0], v[3], v[5] = v[0] + DAMPING, v[3] + DAMPING, v[5] + DAMPING
            factor = cholesky_three(v[:6])
            base = normal_solve(factor, v[6], v[7], v[8])
            table = rows_of(list(factor) + list(base), 16)
            fac[k] = table
            at_obs = lane_gather(table, lands)
            f = [at_obs[i : i + 1] for i in range(6)]
            g = [at_obs[6 + b : 7 + b] for b in range(3)]
            solved = lower_solve(f, *[j0 * ka[b] + j1 * kb[b] for b in range(3)])
            paired = exact_dot(jnp.concatenate(solved, axis=0), match)
            diag = j0 * j0 + j1 * j1
            for b in range(3):
                diag = diag - solved[b] * paired[16 * b : 16 * b + 16]
            w0 = ka[0] * g[0] + ka[1] * g[1] + ka[2] * g[2] - e0
            w1 = kb[0] * g[0] + kb[1] * g[1] + kb[2] * g[2] - e1
            right = j0 * w0 + j1 * w1
            out = exact_dot(jnp.concatenate([right, diag], axis=0), one_cam[k])
            tiles = place(tiles, out, k)
        for i in range(3):
            msg1[i, 0:9, :] = tiles[i][0:9]
            extra = tiles[i][16:32] + damp if i == 0 else tiles[i][16:32]
            msg1[i, 9:18, :] = extra[0:9]

        pl.semaphore_wait(barrier, n_row + n_col - 2)

        hub_of = ((row, hub_col), (2 * col, col), (2 * col + 1, col))

        def contribution(msg, buf, send, recv, i):
            row_slot = lax.rem(col - hub_col + n_col, n_col)
            slot = (
                row_slot if i == 0 else n_col + lax.rem(row - (2 * col + i - 1) + n_row, n_row)
            )
            return pltpu.make_async_remote_copy(
                src_ref=msg.at[i],
                dst_ref=buf.at[slot],
                send_sem=send.at[i],
                recv_sem=recv.at[slot],
                device_id=hub_of[i],
                device_id_type=MESH,
            )

        def not_self(i):
            return jnp.logical_not(is_hub) if i == 0 else row != 2 * col + (i - 1)

        def to_hubs(msg, buf, send, recv):
            for i in range(3):
                @pl.when(not_self(i))
                def _():
                    contribution(msg, buf, send, recv, i).start()

        def sent_to_hubs(msg, buf, send, recv):
            for i in range(3):
                @pl.when(not_self(i))
                def _():
                    contribution(msg, buf, send, recv, i).wait_send()

        def at_hub(msg, buf, send, recv):
            mine_tile = 1 + row - 2 * col
            total = msg[0] + msg[mine_tile]
            for slot in [*range(1, n_col), *range(n_col + 1, n_col + n_row)]:
                pltpu.make_async_remote_copy(
                    src_ref=msg.at[0],
                    dst_ref=buf.at[slot],
                    send_sem=send.at[0],
                    recv_sem=recv.at[slot],
                    device_id=(row, over(1)),
                    device_id_type=MESH,
                ).wait_recv()
            for slot in [*range(1, n_col), *range(n_col + 1, n_col + n_row)]:
                total = total + buf[slot]
            return total

        def spread_copy(buf, send, recv, j):
            mine_tile = 1 + row - 2 * col
            if j < n_col:
                target, slot = (row, over(j)), 0
            else:
                target, slot = (up(j - n_col), col), mine_tile
            return pltpu.make_async_remote_copy(
                src_ref=buf.at[0],
                dst_ref=buf.at[slot],
                send_sem=send.at[j],
                recv_sem=recv.at[slot],
                device_id=target,
                device_id_type=MESH,
            )

        others = [*range(n_col + 1, n_col + n_row), *range(1, n_col)]

        def spread(buf, send, recv):
            for j in others:
                spread_copy(buf, send, recv, j).start()

        def spread_done(buf, send, recv):
            @pl.when(is_hub)
            def _():
                for j in others:
                    spread_copy(buf, send, recv, j).wait_send()

        def arrived(buf, send, recv):
            for i in range(3):
                @pl.when(not_self(i))
                def _():
                    pltpu.make_async_remote_copy(
                        src_ref=buf.at[0],
                        dst_ref=buf.at[i],
                        send_sem=send.at[1],
                        recv_sem=recv.at[i],
                        device_id=(row, over(1)),
                        device_id_type=MESH,
                    ).wait_recv()

        def tile_of(buf, i):
            return rows_of([buf[i]], 16)

        def pushed(vec, k):
            at_obs = lane_gather(vec, oc_ref[k : k + 1, :])
            m0 = col_sum(jac[k, 0] * at_obs)
            m1 = col_sum(jac[k, 1] * at_obs)
            back = [lj_ref[k, b : b + 1, :] * m0 + lj_ref[k, 3 + b : 4 + b, :] * m1 for b in range(3)]
            total = exact_dot(rows_of(back, 16), one_land[k])
            b = [total[i : i + 1] for i in range(3)]
            factor = [fac[k, i : i + 1, :] for i in range(6)]
            return m0, m1, b, normal_solve(factor, *b)

        to_hubs(msg1, in1, s1, r1)

        @pl.when(is_hub)
        def _():
            total = at_hub(msg1, in1, s1, r1)
            z0 = total[0:9] / total[9:18]
            sums[0] = total[0:9]
            sums[1] = total[9:18]
            zbuf[0] = z0
            zbuf[1 + row - 2 * col] = z0
            spread(zbuf, s2, r2)

        arrived(zbuf, s2, r2)

        z_tiles = tuple(tile_of(zbuf, i) for i in range(3))
        zero = jnp.zeros((16, LANES), f32)
        tiles = (damp * z_tiles[0], zero, zero)
        for k in range(n_cl):
            m0, m1, b, y = pushed(vector_of(z_tiles, k), k)
            yvec[k, 0:3, :] = jnp.concatenate(y, axis=0)
            g = lane_gather(rows_of(list(y), 8), ol_ref[k : k + 1, :])
            w0, w1 = m0, m1
            for i in range(3):
                w0 = w0 - lj_ref[k, i : i + 1, :] * g[i : i + 1]
                w1 = w1 - lj_ref[k, 3 + i : 4 + i, :] * g[i : i + 1]
            out = exact_dot(jac[k, 0] * w0 + jac[k, 1] * w1, one_cam[k])
            tiles = place(tiles, out, k)
        for i in range(3):
            msg2[i] = tiles[i][0:9]
        to_hubs(msg2, in2, s3, r3)
        stot[...] = jnp.zeros_like(stot)

        @pl.when(is_hub)
        def _():
            q0 = at_hub(msg2, in2, s3, r3)
            r0, d = sums[0], sums[1]
            t = q0 / d - zbuf[0]
            tbuf[0] = t
            tbuf[1 + row - 2 * col] = t
            spread(tbuf, s4, r4)
            stot[0:1, :] = col_sum(r0 * zbuf[0])
            stot[1:2, :] = col_sum(r0 * t)
            stot[2:3, :] = col_sum(t * d * t)

        arrived(tbuf, s4, r4)

        t_tiles = tuple(tile_of(tbuf, i) for i in range(3))
        form = col_sum(damp * t_tiles[0] * t_tiles[0])
        for k in range(n_cl):
            m0, m1, b, y = pushed(vector_of(t_tiles, k), k)
            yvec[k, 3:6, :] = jnp.concatenate(y, axis=0)
            square = m0 * m0 + m1 * m1
            for at in range(0, n_obs, LANES):
                form = form + square[:, at : at + LANES]
            form = form - (b[0] * y[0] + b[1] * y[1] + b[2] * y[2])
        stot[3:4, :] = form

        def col_copy(i):
            return pltpu.make_async_remote_copy(
                src_ref=stot,
                dst_ref=sc1.at[i],
                send_sem=s5.at[i],
                recv_sem=r5.at[i],
                device_id=(up(i), col),
                device_id_type=MESH,
            )

        def row_copy(i):
            return pltpu.make_async_remote_copy(
                src_ref=sc2.at[0],
                dst_ref=sc2.at[i],
                send_sem=s6.at[i],
                recv_sem=r6.at[i],
                device_id=(row, over(i)),
                device_id_type=MESH,
            )

        for i in range(1, n_row):
            col_copy(i).start()

        def chosen(tile, first_entry, count):
            entry = lax.broadcasted_iota(jnp.int32, (16, LANES), 1) + first_entry
            level = lax.broadcasted_iota(jnp.int32, (16, LANES), 0)
            entry = jnp.minimum(entry, 143)
            cam = entry // 9
            got = gather_rows(tile, cam + 16 * col)
            return col_sum(jnp.where(entry - 9 * cam == level, got, 0.0))[:, :count]

        z_own = jnp.concatenate([chosen(z_tiles[0], 0, 128), chosen(z_tiles[0], 128, 16)], axis=1)
        t_own = jnp.concatenate([chosen(t_tiles[0], 0, 128), chosen(t_tiles[0], 128, 16)], axis=1)

        total = stot[...]
        for i in range(1, n_row):
            col_copy(i).wait_recv()
        for i in range(1, n_row):
            total = total + sc1[i]
        sc2[0] = total
        for i in range(1, n_col):
            row_copy(i).start()
        for i in range(1, n_col):
            row_copy(i).wait_recv()
        for i in range(1, n_col):
            total = total + sc2[i]
        scalars = jnp.sum(total, axis=1, keepdims=True)
        rz, e, f, h = (scalars[i : i + 1] for i in range(4))
        pq = rz + e
        a0 = rz / pq
        new = a0 * ((rz * f - e * e) / pq)
        g = e / pq + new / rz
        curve = g * g * pq - 2.0 * g * a0 * (e + f) + a0 * a0 * h
        a1 = new / curve
        big_a = a0 + a1 * g
        big_b = -a1 * a0
        cam_ref[...] = big_a * z_own + big_b * t_own
        for k in range(n_cl):
            land_ref[k] = -(fac[k, 6:9, :] + big_a * yvec[k, 0:3, :] + big_b * yvec[k, 3:6, :])

        sent_to_hubs(msg1, in1, s1, r1)
        sent_to_hubs(msg2, in2, s3, r3)
        spread_done(zbuf, s2, r2)
        spread_done(tbuf, s4, r4)
        for i in range(1, n_row):
            col_copy(i).wait_send()
        for i in range(1, n_col):
            row_copy(i).wait_send()

    return kernel


def per_device(cam_jac, land_jac, resid, obs_cam, obs_land, pairs, cam_damp):
    n_row = lax.axis_size("row")
    n_col = lax.axis_size("col")
    n_cl, _, n_obs = cam_jac.shape
    shard = cam_damp.shape[0]
    f32 = jnp.float32
    slots = n_row + n_col
    vmem = pl.BlockSpec(memory_space=pltpu.VMEM)
    dma = pltpu.SemaphoreType.DMA
    cam, land = pl.pallas_call(
        make_kernel(n_row, n_col, n_cl, n_obs),
        out_shape=(
            jax.ShapeDtypeStruct((1, shard), f32),
            jax.ShapeDtypeStruct((n_cl, 3, LANES), f32),
        ),
        in_specs=[pl.BlockSpec(memory_space=pltpu.SMEM)] + [vmem] * 6,
        out_specs=(vmem, vmem),
        scratch_shapes=[
            pltpu.VMEM((n_cl, 2, 16, n_obs), f32),
            pltpu.VMEM((n_cl, n_obs, LANES), jnp.bfloat16),
            pltpu.VMEM((n_cl, n_obs, LANES), jnp.bfloat16),
            pltpu.VMEM((n_cl, 16, LANES), f32),
            pltpu.VMEM((n_cl, 8, LANES), f32),
            pltpu.VMEM((3, 18, LANES), f32),
            pltpu.VMEM((3, 9, LANES), f32),
            pltpu.VMEM((2, 9, LANES), f32),
            pltpu.VMEM((slots, 18, LANES), f32),
            pltpu.VMEM((slots, 9, LANES), f32),
            pltpu.VMEM((3, 9, LANES), f32),
            pltpu.VMEM((3, 9, LANES), f32),
            pltpu.VMEM((n_row, 4, LANES), f32),
            pltpu.VMEM((n_col, 4, LANES), f32),
            pltpu.VMEM((4, LANES), f32),
            dma((3,)), dma((slots,)),
            dma((slots,)), dma((3,)),
            dma((3,)), dma((slots,)),
            dma((slots,)), dma((3,)),
            dma((n_row,)), dma((n_row,)),
            dma((n_col,)), dma((n_col,)),
        ],
        compiler_params=pltpu.CompilerParams(collective_id=0, has_side_effects=True),
        name="schur_step",
    )(pairs, cam_jac, land_jac, resid, obs_cam, obs_land, cam_damp.reshape(1, shard))
    return cam.reshape(shard), land


def solution(mesh):
    in_specs = (
        P(("row", "col"), None, None),
        P(("row", "col"), None, None),
        P(("row", "col"), None, None),
        P(("row", "col"), None),
        P(("row", "col"), None),
        P(("row", "col"), None),
        P(("row", "col")),
    )
    out_specs = (P(("row", "col")), P(("row", "col"), None, None))
    return jax.shard_map(
        per_device, mesh=mesh, in_specs=in_specs, out_specs=out_specs, check_vma=False
    )
```

time: 1580 us -> 47.4 us (0.03); the launches traced: 1560 us -> 47.1 us
  waiting for transfers between devices: 664 us -> 0 us
  local copies, waits for them, and re-layouts: 363 us -> 6.25 us
  blocking collectives: 278 us -> 0 us
  matrix products: 143 us -> 0 us
  other arithmetic: 87 us -> 0 us
  Pallas kernels: 0 us -> 40.2 us
  between operations: 26.5 us -> 0.66 us
    unnamed x13 -> x0, waiting for transfers between devices: 664 us -> none
    psum x4 -> x0, blocking collectives: 250 us -> none  [the longest x2 127 us: residual_weight(): return lax.psum(jnp.sum(residual * precon_res), ('row', 'col'))]
    mul x38 -> x0, local copies, waits for them, and re-layouts: 145 us -> none  [the longest x16 74.6 us: cluster_schur(): eye_cam[:, None, :, None] * blocks[0][:, :, None, :]]
    dot_general x50 -> x0, matrix products: 143 us -> none  [the longest x2 23.7 us: per_device(): forward = jnp.dot(grid, col_part, precision=HIGHEST)]
    dynamic_update_slice x15 -> x0, local copies, waits for them, and re-layouts: 124 us -> none  [the longest x12 121 us: add_block(): lax.dynamic_update_slice(target, current + block, (row_start, col_start))]
    mul x25 -> x0, other arithmetic: 54.2 us -> none  [the longest x1 51.1 us: cluster_schur(): eye_cam[:, None, :, None] * blocks[1][:, :, None, :]]
    pallas_call x0 -> x1, Pallas kernels: none -> 40.2 us  [per_device(): pl.pallas_call(make_kernel(n_row, n_col, n_cl, n_obs), out_shape=(jax.Sha...]
    slice x30 -> x0, local copies, waits for them, and re-layouts: 29.8 us -> none  [the longest x12 13.8 us: cluster_schur(): coupling_second = coupling[width:]]
  transfers between devices with their start and end apart: 7 -> 0, of which waited for: 5 -> 0; matrix products, arithmetic and copies ran while one was open for 17% -> 0% of each run, Pallas kernels for 0% -> 0%
where the time goes in v1:
time: 47.4 us; the launch traced here: 47.1 us
  Pallas kernels  40.2 us (85%)
  local copies, waits for them, and re-layouts  6.25 us (13%)
  between operations  0.66 us (1%)
    pallas_call x1, Pallas kernels, per_device(): pl.pallas_call(make_kernel(n_row, n_col, n_cl, n_obs), out_shape=(jax.Sha...  40.2 us
    unnamed x9, local copies, waits for them, and re-layouts  6.25 us

profile of v1, /device:TPU:1, one launch (start us, length us, event | category | flops | bytes accessed | tf_op | source)
XLA Modules:
  0.0 47.1 jit_solution(14768238954954130151)
XLA Ops:
  0.6 0.0 copy-start
  0.6 0.7 %copy-done = s32[4,2]{0,1:T(2,128)S(1)} copy-done((s32[4,2]{0,1:T(2,128)S(1)}, s32[4,2]{0,1:T(2,128)}, u32[]{:S(2)}) %copy-start) | copy-done | bytes 56
  1.3 0.7 %copy.9.pairs_ref = s32[4,2]{1,0:T(4,128)} copy(s32[4,2]{0,1:T(2,128)S(1)} %copy-done) | data formatting | bytes 64 | tf_op args[5]
  2.0 1.4 %copy.11.lj_ref = f32[4,6,512]{2,1,0:T(8,128)} copy(f32[4,6,512]{2,0,1:T(4,128)} %param.8) | data formatting | bytes 98304 | tf_op args[1]
  3.4 1.6 %copy.10.cj_ref = f32[4,18,512]{2,1,0:T(8,128)} copy(f32[4,18,512]{2,0,1:T(4,128)} %param.7) | data formatting | bytes 294912 | tf_op args[0]
  5.0 40.2 %schur_step.1 = (f32[1,144]{1,0:T(1,128)}, f32[4,3,128]{2,1,0:T(4,128)}) custom-call(s32[4,2]{1,0:T(4,128)} %copy.9.pairs_ref, f32[4,18,512]{2,1,0:T(8,128)} %copy.10.cj_ref, f32[4,6,512]{2,1,0:T(8,128)} %copy.11.lj_ref, f32[4,2,512]{2,1,0:T(2,128)} %re_ref.1, s32[4,512]{1,0:T(4,128)} %oc_ref.1, s32[4,512]{1,0:T(4,128)} %ol_ref.1, f32[1,144]{1,0:T(1,128)} %bitcast.2), custom_call_target="tpu_custom_call" | custom-call | tf_op jit(solution)/shard_map/schur_step/pallas_call | solution.py:450
  45.2 0.0 copy-start.1
  45.2 1.3 %copy.12 = f32[4,3,128]{2,0,1:T(4,128)} copy(f32[4,3,128]{2,1,0:T(4,128)} %get-tuple-element.7) | data formatting | bytes 12288
  46.5 0.0 copy-done.1
  46.5 0.6 %copy.14 = f32[144]{0:T(256)} copy(f32[144]{0:T(256)S(1)} %bitcast.3) | data formatting | bytes 1152
Async XLA Ops:
  0.6 0.7 %copy-start = (s32[4,2]{0,1:T(2,128)S(1)}, s32[4,2]{0,1:T(2,128)}, u32[]{:S(2)}) copy-start(s32[4,2]{0,1:T(2,128)} %param.12) | copy-start | bytes 100
  45.2 1.3 %copy-start.1 = (f32[1,144]{1,0:T(1,128)S(1)}, f32[1,144]{1,0:T(1,128)}, u32[]{:S(2)}) copy-start(f32[1,144]{1,0:T(1,128)} %get-tuple-element.4) | copy-start | bytes 1732

commit v2 on v1

v2 whole, which is shorter than its diff:
```python
import jax
import jax.numpy as jnp
from jax import lax
from jax.experimental import pallas as pl
from jax.experimental.pallas import tpu as pltpu
from jax.sharding import PartitionSpec as P

DAMPING = 1.0
MESH = pl.DeviceIdType.MESH
LANES = 128
SIDE = 4
VMEM = 8 << 20


def lane_gather(table, index):
    dims = lax.GatherDimensionNumbers((), (1,), (1,), (0,), (0,))
    pieces = [
        lax.gather(
            table,
            index[at : at + 8, :, None],
            dims,
            slice_sizes=(1, 1),
            mode=lax.GatherScatterMode.PROMISE_IN_BOUNDS,
        )
        for at in range(0, index.shape[0], 8)
    ]
    return pieces[0] if len(pieces) == 1 else jnp.concatenate(pieces, axis=0)


def three_parts(x):
    high = x.astype(jnp.bfloat16).astype(jnp.float32)
    rest = x - high
    mid = rest.astype(jnp.bfloat16).astype(jnp.float32)
    return high, mid, rest - mid


def dot_nt(x, onehot):
    return lax.dot_general(
        x, onehot, (((1,), (1,)), ((), ())), preferred_element_type=jnp.float32
    )


def stacked_parts(x):
    high = x.astype(jnp.bfloat16)
    rest = x - high.astype(jnp.float32)
    mid = rest.astype(jnp.bfloat16)
    low = (rest - mid.astype(jnp.float32)).astype(jnp.bfloat16)
    return jnp.concatenate([high, mid, low], axis=0)


def add_parts(out):
    rows = out.shape[0] // 3
    return out[:rows] + (out[rows : 2 * rows] + out[2 * rows :])


def col_sum(x):
    return jnp.sum(x, axis=0, keepdims=True)


def lower_solve(f, a, b, c):
    one = a * f[0]
    two = (b - f[1] * one) * f[3]
    three = (c - f[2] * one - f[4] * two) * f[5]
    return one, two, three


def upper_solve(f, a, b, c):
    three = c * f[5]
    two = (b - f[4] * three) * f[3]
    one = (a - f[1] * two - f[2] * three) * f[0]
    return one, two, three


def normal_solve(f, a, b, c):
    return upper_solve(f, *lower_solve(f, a, b, c))


def cholesky_three(v):
    inv_first = 1.0 / jnp.sqrt(v[0])
    low_one = v[1] * inv_first
    low_two = v[2] * inv_first
    inv_second = 1.0 / jnp.sqrt(v[3] - low_one * low_one)
    low_three = (v[4] - low_two * low_one) * inv_second
    inv_third = 1.0 / jnp.sqrt(v[5] - low_two * low_two - low_three * low_three)
    return inv_first, low_one, low_two, inv_second, low_three, inv_third


def make_kernel(n_row, n_col, n_cl, n_obs):
    f32 = jnp.float32

    tiles_n = n_obs // LANES
    dense = tiles_n * n_cl

    def kernel(
        pairs_in, cj_in, lj_in, re_in, oc_in, ol_in, damp_in,
        cam_ref, land_ref,
        pairs_ref, cj_ref, lj_ref, re_ref, oc_ref, ol_ref, damp_ref, s0,
        one_cam, one_land, ustat, wstat, xstat, bstat, res, vecs, fac, yvec,
        msg1, msg2, sums, in1, in2, zbuf, tbuf, own, stot,
        s1, r1, s2, r2, s3, r3, s4, r4, s5, r5,
    ):
        one = jnp.asarray(1, jnp.bfloat16)
        nil = jnp.asarray(0, jnp.bfloat16)
        row = lax.axis_index("row")
        col = lax.axis_index("col")
        hub_col = row // 2
        is_hub = col == hub_col
        z, x = row // SIDE, lax.rem(row, SIDE)
        zs = [lax.rem(z + d, SIDE) * SIDE for d in range(SIDE)]
        xs = [lax.rem(x + d, SIDE) for d in range(SIDE)]
        cols = [lax.rem(col + d, n_col) for d in range(n_col)]
        up = lambda i: zs[i // SIDE] + xs[i % SIDE]
        over = lambda i: cols[i]

        def apart(i):
            return sum(min(d, SIDE - d) for d in (i // SIDE, i % SIDE))

        plane = sorted(range(1, n_row), key=lambda i: -apart(i))
        ring = [*range(2, n_col - 1), 1, n_col - 1]

        loads = [
            pltpu.make_async_copy(source, target, s0.at[n])
            for n, (source, target) in enumerate(
                (
                    (oc_in, oc_ref),
                    (ol_in, ol_ref),
                    (lj_in, lj_ref),
                    (re_in, re_ref),
                    (cj_in, cj_ref),
                    (pairs_in, pairs_ref),
                    (damp_in, damp_ref),
                )
            )
        ]
        for load in loads:
            load.start()

        barrier = pltpu.get_barrier_semaphore()

        @pl.when(is_hub)
        def _():
            for i in plane:
                pl.semaphore_signal(barrier, inc=1, device_id=(up(i), col), device_id_type=MESH)
            for i in range(1, n_col):
                pl.semaphore_signal(barrier, inc=1, device_id=(row, over(i)), device_id_type=MESH)

        def place(tiles, out, k):
            rolled = pltpu.roll(out, 64, axis=1)
            half = lax.broadcasted_iota(jnp.int32, out.shape, 1) < 64

            def pick(cond, x):
                return jnp.where(cond, x, 0.0)

            a, b = first[k], second[k]
            return (
                tiles[0] + jnp.where(half, pick(a == 0, out), pick(a == 1, rolled)),
                tiles[1] + jnp.where(half, pick(b == 0, rolled), pick(b == 1, out)),
                tiles[2] + jnp.where(half, pick(b == 2, rolled), pick(b == 3, out)),
            )

        def jac(r, a):
            return cj_ref[(r * 9 + a) * dense : (r * 9 + a + 1) * dense, :]

        def land_jac(r, b):
            return lj_ref[(r * 3 + b) * dense : (r * 3 + b + 1) * dense, :]

        def put(ref, q, value):
            ref[q * dense : (q + 1) * dense, :] = value

        def of_cluster(ref, k, rows):
            return jnp.concatenate(
                [ref[pl.ds(j * n_cl + k, rows, stride=dense), :] for j in range(tiles_n)], axis=1
            )

        def put_result(k, value):
            rows = value.shape[0]
            res[k * 32 : k * 32 + rows, :] = value
            res[(k + n_cl) * 32 : (k + n_cl) * 32 + rows, :] = value

        def result(q):
            return res[pl.ds(q, 2 * n_cl, stride=32), :]

        loads[0].wait()
        loads[1].wait()
        cams = oc_ref[...]
        lands = ol_ref[...]

        cams_f = cams.astype(f32)
        lands_f = lands.astype(f32)

        def packed_row(x, j, k):
            at = j * n_cl + k
            return jnp.broadcast_to(x[at : at + 1, :], (16, LANES)).astype(jnp.bfloat16)

        level = [
            (lax.broadcasted_iota(jnp.int32, (16, LANES), 0) + 16 * i).astype(f32).astype(jnp.bfloat16)
            for i in range(8)
        ]
        for k in range(n_cl):
            for j in range(tiles_n):
                land_row = packed_row(lands_f, j, k)
                cam_row = packed_row(cams_f, j, k)
                for i in range(8):
                    at = (k, slice(16 * i, 16 * i + 16), slice(j * LANES, (j + 1) * LANES))
                    one_land[at] = jnp.where(level[i] == land_row, one, nil)
                    one_cam[at] = jnp.where(level[i] == cam_row, one, nil)

        power = jnp.full((dense, LANES), 2.0**-64, f32)
        for i in range(7):
            power = power * jnp.where(((cams >> i) & 1) == 1, 2.0 ** (2**i), 1.0)
        code = power * (1.0 + lands_f * (1.0 / 128.0))
        code_t = code.T

        zero = jnp.zeros((dense, LANES), f32)
        for q in range(27, 32):
            put(xstat, q, zero)
            put(ustat, q, zero)
        for q in range(18, 24):
            put(wstat, q, zero)
        for q in range(9, 16):
            put(bstat, q, zero)
        loads[2].wait()
        loads[3].wait()
        ka = [land_jac(0, b) for b in range(3)]
        kb = [land_jac(1, b) for b in range(3)]
        e0, e1 = (
            jnp.concatenate(
                [re_ref[pl.ds(2 * j + r, n_cl, stride=2 * tiles_n), :] for j in range(tiles_n)], axis=0
            )
            for r in range(2)
        )
        stats = [
            ka[i] * ka[j] + kb[i] * kb[j]
            for i, j in ((0, 0), (0, 1), (0, 2), (1, 1), (1, 2), (2, 2))
        ] + [ka[b] * e0 + kb[b] * e1 for b in range(3)]
        for q, stat in enumerate(stats):
            for p, part in enumerate(three_parts(stat)):
                put(xstat, p * 9 + q, part)
        for k in range(n_cl):
            put_result(k, dot_nt(of_cluster(xstat, k, 32).astype(jnp.bfloat16), one_land[k]))
        v = [result(q) + (result(9 + q) + result(18 + q)) for q in range(9)]
        v[0], v[3], v[5] = v[0] + DAMPING, v[3] + DAMPING, v[5] + DAMPING
        factor = cholesky_three(v[:6])
        base = normal_solve(factor, v[6], v[7], v[8])
        for i in range(6):
            fac[i] = factor[i]
        for b in range(3):
            yvec[b] = base[b]

        loads[4].wait()
        loads[5].wait()
        loads[6].wait()
        first = [pairs_ref[0, k] - 2 * row for k in range(n_cl)]
        second = [pairs_ref[1, k] - 4 * col for k in range(n_cl)]

        lane = lax.broadcasted_iota(jnp.int32, (16, LANES), 1)
        sub = lax.broadcasted_iota(jnp.int32, (16, LANES), 0)
        flat = (lane - 16 * col) * 9 + sub
        mine = (lane >= 16 * col) & (lane < 16 * col + 16) & (sub < 9)
        flat = jnp.where(mine, flat, 0)
        damp_low = jnp.broadcast_to(damp_ref[:, :LANES], (8, LANES))
        damp_high = jnp.broadcast_to(
            jnp.concatenate([damp_ref[:, LANES:], jnp.zeros((1, 2 * LANES - 144), f32)], axis=1),
            (8, LANES),
        )
        damp = jnp.where(
            flat < LANES,
            lane_gather(damp_low, jnp.minimum(flat, LANES - 1)),
            lane_gather(damp_high, jnp.maximum(flat - LANES, 0)),
        )
        damp = jnp.where(mine, damp, 0.0)

        f = [lane_gather(factor[i], lands) for i in range(6)]
        g = [lane_gather(base[b], lands) for b in range(3)]
        w0 = ka[0] * g[0] + ka[1] * g[1] + ka[2] * g[2] - e0
        w1 = kb[0] * g[0] + kb[1] * g[1] + kb[2] * g[2] - e1
        for a in range(9):
            j0, j1 = jac(0, a), jac(1, a)
            solved = lower_solve(f, *[j0 * ka[b] + j1 * kb[b] for b in range(3)])
            for b in range(3):
                put(ustat, b * 8 + a if a < 8 else 24 + b, solved[b])
            put(wstat, a if a < 8 else 16, j0 * w0 + j1 * w1)
            put(wstat, 8 + a if a < 8 else 17, j0 * j0 + j1 * j1)
        zero = jnp.zeros((32, LANES), f32)
        tiles = (zero, zero, zero)
        for k in range(n_cl):
            rows_packed = [
                jnp.concatenate([packed_row(code, j, k)] * 8, axis=0) for j in range(tiles_n)
            ]
            blocks = []
            for j in range(tiles_n):
                at = j * n_cl + k
                column = jnp.broadcast_to(code_t[:, at : at + 1], (LANES, LANES)).astype(jnp.bfloat16)
                blocks.append(
                    jnp.concatenate([jnp.where(column == r, one, nil) for r in rows_packed], axis=1)
                )
            match = jnp.concatenate(blocks, axis=0)
            solved = of_cluster(ustat, k, 32)
            paired = add_parts(
                jnp.dot(stacked_parts(solved), match, preferred_element_type=jnp.float32)
            )
            square = solved * paired
            plain = of_cluster(wstat, k, 24)
            diag = plain[8:16] - (square[0:8] + square[8:16] + square[16:24])
            lhs = jnp.concatenate([plain[0:8], diag, plain[16:24], square[24:32]], axis=0)
            tiles = place(tiles, add_parts(dot_nt(stacked_parts(lhs), one_cam[k])), k)
        for i in range(3):
            extra = damp if i == 0 else jnp.zeros((16, LANES), f32)
            t = tiles[i]
            msg1[i, 0:8, :] = t[0:8]
            msg1[i, 8:16, :] = t[8:16] + extra[0:8]
            msg1[i, 16:17, :] = t[16:17]
            msg1[i, 17:18, :] = t[17:18] - (t[24:25] + t[25:26] + t[26:27]) + extra[8:9]

        pl.semaphore_wait(barrier, jnp.where(is_hub, 1, 3))

        hub_of = ((row, hub_col), (2 * col, col), (2 * col + 1, col))

        def contribution(msg, buf, send, recv, i):
            row_slot = lax.rem(col - hub_col + n_col, n_col)
            hub_z, hub_x = (2 * col + i - 1) // SIDE, lax.rem(2 * col + i - 1, SIDE)
            plane_slot = lax.rem(z - hub_z + SIDE, SIDE) * SIDE + lax.rem(x - hub_x + SIDE, SIDE)
            slot = row_slot if i == 0 else n_col + plane_slot
            return pltpu.make_async_remote_copy(
                src_ref=msg.at[i],
                dst_ref=buf.at[slot],
                send_sem=send.at[i],
                recv_sem=recv.at[slot],
                device_id=hub_of[i],
                device_id_type=MESH,
            )

        def not_self(i):
            return jnp.logical_not(is_hub) if i == 0 else row != 2 * col + (i - 1)

        def to_hubs(msg, buf, send, recv):
            for i in range(3):
                @pl.when(not_self(i))
                def _():
                    contribution(msg, buf, send, recv, i).start()

        def sent_to_hubs(msg, buf, send, recv):
            for i in range(3):
                @pl.when(not_self(i))
                def _():
                    contribution(msg, buf, send, recv, i).wait_send()

        def at_hub(msg, buf, send, recv):
            mine_tile = 1 + row - 2 * col
            total = msg[0] + msg[mine_tile]
            late = [n_col + i for i in plane[::-1]]
            for slot in [*ring, *late]:
                pltpu.make_async_remote_copy(
                    src_ref=msg.at[0],
                    dst_ref=buf.at[slot],
                    send_sem=send.at[0],
                    recv_sem=recv.at[slot],
                    device_id=(row, over(1)),
                    device_id_type=MESH,
                ).wait_recv()
            for slot in [*ring, *late]:
                total = total + buf[slot]
            return total

        def spread_copy(buf, send, recv, j):
            mine_tile = 1 + row - 2 * col
            if j < n_col:
                target, slot = (row, over(j)), 0
            else:
                target, slot = (up(j - n_col), col), mine_tile
            return pltpu.make_async_remote_copy(
                src_ref=buf.at[0],
                dst_ref=buf.at[slot],
                send_sem=send.at[j],
                recv_sem=recv.at[slot],
                device_id=target,
                device_id_type=MESH,
            )

        others = [*[n_col + i for i in plane], *ring]

        def spread(buf, send, recv):
            for j in others:
                spread_copy(buf, send, recv, j).start()

        def spread_done(buf, send, recv):
            @pl.when(is_hub)
            def _():
                for j in others:
                    spread_copy(buf, send, recv, j).wait_send()

        def arrived(buf, send, recv):
            for i in range(3):
                @pl.when(not_self(i))
                def _():
                    pltpu.make_async_remote_copy(
                        src_ref=buf.at[0],
                        dst_ref=buf.at[i],
                        send_sem=send.at[1],
                        recv_sem=recv.at[i],
                        device_id=(row, over(1)),
                        device_id_type=MESH,
                    ).wait_recv()

        left = lax.broadcasted_iota(jnp.int32, (9, LANES), 1) < 64

        def pushed(tiles):
            rolled = [pltpu.roll(t, 64, axis=1) for t in tiles]
            for k in range(n_cl):
                a, b = first[k], second[k]
                own = jnp.where(a == 0, tiles[0], rolled[0])
                odd = jnp.where(b < 2, tiles[1], tiles[2])
                even = jnp.where(b < 2, rolled[1], rolled[2])
                vec = jnp.where(left, own, jnp.where((b == 1) | (b == 3), odd, even))
                vecs[k * 16 : k * 16 + 9, :] = vec
                vecs[(k + n_cl) * 16 : (k + n_cl) * 16 + 9, :] = vec
            m0 = m1 = None
            for a in range(9):
                at_obs = lane_gather(vecs[pl.ds(a, 2 * n_cl, stride=16), :], cams)
                p0, p1 = jac(0, a) * at_obs, jac(1, a) * at_obs
                m0, m1 = (p0, p1) if m0 is None else (m0 + p0, m1 + p1)
            for b in range(3):
                back = land_jac(0, b) * m0 + land_jac(1, b) * m1
                for p, part in enumerate(three_parts(back)):
                    put(bstat, p * 3 + b, part)
            for k in range(n_cl):
                put_result(k, dot_nt(of_cluster(bstat, k, 16).astype(jnp.bfloat16), one_land[k]))
            total = [result(b) + (result(3 + b) + result(6 + b)) for b in range(3)]
            return m0, m1, total, normal_solve([fac[i] for i in range(6)], *total)

        to_hubs(msg1, in1, s1, r1)

        @pl.when(is_hub)
        def _():
            total = at_hub(msg1, in1, s1, r1)
            sums[...] = total
            zbuf[0, 0:8, :] = total[0:8] / total[8:16]
            zbuf[0, 8:9, :] = total[16:17] / total[17:18]
            spread(zbuf, s2, r2)
            zbuf[1 + row - 2 * col] = zbuf[0]

        arrived(zbuf, s2, r2)

        z_tiles = tuple(zbuf[i] for i in range(3))
        m0, m1, b, y = pushed(z_tiles)
        for i in range(3):
            yvec[3 + i] = y[i]
        w0, w1 = m0, m1
        for i in range(3):
            g = lane_gather(y[i], lands)
            w0 = w0 - land_jac(0, i) * g
            w1 = w1 - land_jac(1, i) * g
        for a in range(9):
            for p, part in enumerate(three_parts(jac(0, a) * w0 + jac(1, a) * w1)):
                put(xstat, p * 8 + a if a < 8 else 24 + p, part)
        zero = jnp.zeros((16, LANES), f32)
        tiles = (zero, zero, zero)
        for k in range(n_cl):
            out = dot_nt(of_cluster(xstat, k, 32).astype(jnp.bfloat16), one_cam[k])
            out = jnp.concatenate([out[0:8] + (out[8:16] + out[16:24]), out[24:32]], axis=0)
            tiles = place(tiles, out, k)
        for i in range(3):
            t = tiles[i]
            low, high = t[0:8], t[8:9] + (t[9:10] + t[10:11])
            if i == 0:
                low = low + damp[0:8] * z_tiles[0][0:8]
                high = high + damp[8:9] * z_tiles[0][8:9]
            msg2[i, 0:8, :] = low
            msg2[i, 8:9, :] = high
        to_hubs(msg2, in2, s3, r3)
        own[...] = jnp.zeros_like(own)

        @pl.when(is_hub)
        def _():
            q0 = at_hub(msg2, in2, s3, r3)
            total = sums[...]
            d_low, d_high = total[8:16], total[17:18]
            z_low, z_high = zbuf[0, 0:8, :], zbuf[0, 8:9, :]
            t_low = q0[0:8] / d_low - z_low
            t_high = q0[8:9] / d_high - z_high
            tbuf[0, 0:8, :] = t_low
            tbuf[0, 8:9, :] = t_high
            spread(tbuf, s4, r4)
            tbuf[1 + row - 2 * col] = tbuf[0]
            r_low, r_high = total[0:8], total[16:17]
            own[0:1, :] = col_sum(r_low * z_low) + r_high * z_high
            own[1:2, :] = col_sum(r_low * t_low) + r_high * t_high
            own[2:3, :] = col_sum(t_low * d_low * t_low) + t_high * d_high * t_high

        arrived(tbuf, s4, r4)

        t_tiles = tuple(tbuf[i] for i in range(3))
        m0, m1, b, y = pushed(t_tiles)
        for i in range(3):
            yvec[6 + i] = y[i]
        square = m0 * m0 + m1 * m1
        form = -0.5 * (b[0] * y[0] + b[1] * y[1] + b[2] * y[2])
        for at in range(0, dense, 8):
            form = form + square[at : at + 8]
        t = t_tiles[0]
        form = form + damp[0:8] * t[0:8] * t[0:8]
        own[3:4, :] = col_sum(form) + damp[8:9] * t[8:9] * t[8:9]

        quarter = lax.broadcasted_iota(jnp.int32, (4, LANES), 1) // 32
        which = lax.broadcasted_iota(jnp.int32, (4, LANES), 0)
        four = own[...]
        four = four + pltpu.roll(four, 64, axis=1)
        four = four + pltpu.roll(four, 32, axis=1)
        stot[0:1, :] = col_sum(jnp.where(quarter == which, four, 0.0))

        def total_copy(i, j):
            slot = i * n_col + j
            return pltpu.make_async_remote_copy(
                src_ref=stot.at[pl.ds(0, 1)],
                dst_ref=stot.at[pl.ds(slot, 1)],
                send_sem=s5,
                recv_sem=r5,
                device_id=(up(i), over(j)),
                device_id_type=MESH,
            )

        def total_wait():
            return pltpu.make_async_remote_copy(
                src_ref=stot.at[pl.ds(1, n_row * n_col - 1)],
                dst_ref=stot.at[pl.ds(1, n_row * n_col - 1)],
                send_sem=s5,
                recv_sem=r5,
                device_id=(row, over(1)),
                device_id_type=MESH,
            )

        far = sorted(
            [(i, j) for i in range(n_row) for j in range(n_col) if i or j],
            key=lambda ij: -(apart(ij[0]) + min(ij[1], n_col - ij[1]) / 2),
        )
        for i, j in far:
            total_copy(i, j).start()

        def chosen(tile, first_entry, count):
            entry = lax.broadcasted_iota(jnp.int32, (8, LANES), 1) + first_entry
            level = lax.broadcasted_iota(jnp.int32, (8, LANES), 0)
            entry = jnp.minimum(entry, 143)
            cam = entry // 9
            rest = entry - 9 * cam
            at = cam + 16 * col
            low = jnp.where(rest == level, lane_gather(tile[0:8], at), 0.0)
            high = lane_gather(jnp.broadcast_to(tile[8:9], (8, LANES)), at)
            return col_sum(low + jnp.where((rest == 8) & (level == 0), high, 0.0))[:, :count]

        z_own = jnp.concatenate([chosen(z_tiles[0], 0, 128), chosen(z_tiles[0], 128, 16)], axis=1)
        t_own = jnp.concatenate([chosen(t_tiles[0], 0, 128), chosen(t_tiles[0], 128, 16)], axis=1)

        sent_to_hubs(msg1, in1, s1, r1)
        sent_to_hubs(msg2, in2, s3, r3)
        spread_done(zbuf, s2, r2)
        spread_done(tbuf, s4, r4)
        total_wait().wait_recv()
        total = jnp.where(quarter == which, col_sum(stot[...]), 0.0)
        scalars = jnp.sum(total, axis=1, keepdims=True)
        rz, e, f, h = (scalars[i : i + 1] for i in range(4))
        pq = rz + e
        a0 = rz / pq
        new = a0 * ((rz * f - e * e) / pq)
        g = e / pq + new / rz
        curve = g * g * pq - 2.0 * g * a0 * (e + f) + a0 * a0 * h
        a1 = new / curve
        big_a = a0 + a1 * g
        big_b = -a1 * a0
        cam_ref[...] = big_a * z_own + big_b * t_own
        for b in range(3):
            land = -(yvec[b] + big_a * yvec[3 + b] + big_b * yvec[6 + b])
            land_ref[b] = land[0:n_cl]
        total_wait().wait_send()

    return kernel


def per_device(cam_jac, land_jac, resid, obs_cam, obs_land, pairs, cam_damp):
    n_row = lax.axis_size("row")
    n_col = lax.axis_size("col")
    n_cl, _, n_obs = cam_jac.shape
    shard = cam_damp.shape[0]
    f32 = jnp.float32
    slots = n_row + n_col
    tiles = n_obs // LANES
    dense = n_cl * tiles
    vmem = pl.BlockSpec(memory_space=pltpu.VMEM)
    dma = pltpu.SemaphoreType.DMA

    def entries_first(x):
        return (
            x.reshape(n_cl, -1, tiles, LANES).transpose(1, 2, 0, 3).reshape(-1, LANES)
        )

    cam, land = pl.pallas_call(
        make_kernel(n_row, n_col, n_cl, n_obs),
        out_shape=(
            jax.ShapeDtypeStruct((1, shard), f32),
            jax.ShapeDtypeStruct((3, n_cl, LANES), f32),
        ),
        in_specs=[pl.BlockSpec(memory_space=pltpu.HBM)] * 7,
        out_specs=(vmem, vmem),
        scratch_shapes=[
            pltpu.SMEM((2, n_cl), jnp.int32),
            pltpu.VMEM((18 * dense, LANES), f32),
            pltpu.VMEM((6 * dense, LANES), f32),
            pltpu.VMEM((2 * dense, LANES), f32),
            pltpu.VMEM((dense, LANES), jnp.int32),
            pltpu.VMEM((dense, LANES), jnp.int32),
            pltpu.VMEM((1, shard), f32),
            dma((7,)),
            pltpu.VMEM((n_cl, LANES, n_obs), jnp.bfloat16),
            pltpu.VMEM((n_cl, LANES, n_obs), jnp.bfloat16),
            pltpu.VMEM((32 * dense, LANES), f32),
            pltpu.VMEM((24 * dense, LANES), f32),
            pltpu.VMEM((32 * dense, LANES), f32),
            pltpu.VMEM((16 * dense, LANES), f32),
            pltpu.VMEM((2 * n_cl * 32, LANES), f32),
            pltpu.VMEM((2 * n_cl * 16, LANES), f32),
            pltpu.VMEM((6, 8, LANES), f32),
            pltpu.VMEM((9, 8, LANES), f32),
            pltpu.VMEM((3, 18, LANES), f32),
            pltpu.VMEM((3, 9, LANES), f32),
            pltpu.VMEM((18, LANES), f32),
            pltpu.VMEM((slots, 18, LANES), f32),
            pltpu.VMEM((slots, 9, LANES), f32),
            pltpu.VMEM((3, 9, LANES), f32),
            pltpu.VMEM((3, 9, LANES), f32),
            pltpu.VMEM((4, LANES), f32),
            pltpu.VMEM((n_row * n_col, LANES), f32),
            dma((3,)), dma((slots,)),
            dma((slots,)), dma((3,)),
            dma((3,)), dma((slots,)),
            dma((slots,)), dma((3,)),
            dma, dma,
        ],
        compiler_params=pltpu.CompilerParams(collective_id=0, has_side_effects=True, vmem_limit_bytes=VMEM),
        name="schur_step",
    )(
        *(
            pltpu.with_memory_space_constraint(x, pltpu.HBM)
            for x in (
        pairs.T,
        entries_first(cam_jac),
        entries_first(land_jac),
        resid.reshape(n_cl, 2, tiles, LANES).transpose(0, 2, 1, 3).reshape(-1, LANES),
        obs_cam.reshape(n_cl, tiles, LANES).transpose(1, 0, 2).reshape(-1, LANES),
        obs_land.reshape(n_cl, tiles, LANES).transpose(1, 0, 2).reshape(-1, LANES),
        cam_damp.reshape(1, shard),
            )
        )
    )
    return cam.reshape(shard), land.transpose(1, 0, 2)


def solution(mesh):
    in_specs = (
        P(("row", "col"), None, None),
        P(("row", "col"), None, None),
        P(("row", "col"), None, None),
        P(("row", "col"), None),
        P(("row", "col"), None),
        P(("row", "col"), None),
        P(("row", "col")),
    )
    out_specs = (P(("row", "col")), P(("row", "col"), None, None))
    return jax.shard_map(
        per_device, mesh=mesh, in_specs=in_specs, out_specs=out_specs, check_vma=False
    )
```

time: 47.4 us -> 36.7 us (0.77)
  Pallas kernels: 40.2 us -> 34.8 us
  local copies, waits for them, and re-layouts: 6.25 us -> 1.16 us
    pallas_call x1, Pallas kernels: 40.2 us -> 34.8 us  [per_device(): pl.pallas_call(make_kernel(n_row, n_col, n_cl, n_obs), out_shape=(jax.Sha...]
    unnamed x9 -> x2, local copies, waits for them, and re-layouts: 6.25 us -> 1.16 us
where the time goes in v2:
time: 36.7 us; the launch traced here: 36.5 us
  Pallas kernels  34.8 us (95%)
  local copies, waits for them, and re-layouts  1.16 us (3%)
  between operations  0.64 us (2%)
    pallas_call x1, Pallas kernels, per_device(): pl.pallas_call(make_kernel(n_row, n_col, n_cl, n_obs), out_shape=(jax.Sha...  34.8 us
    unnamed x2, local copies, waits for them, and re-layouts  1.16 us

profile of v2, /device:TPU:1, one launch (start us, length us, event | category | flops | bytes accessed | tf_op | source)
XLA Modules:
  0.0 36.5 jit_solution(3712174523978376807)
XLA Ops:
  0.6 34.8 %schur_step.1 = (f32[1,144]{1,0:T(1,128)S(1)}, f32[3,4,128]{2,1,0:T(4,128)S(1)}) custom-call(s32[2,4]{1,0:T(2,128)} %bitcast.36, f32[288,128]{1,0:T(8,128)} %bitcast.31, f32[96,128]{1,0:T(8,128)} %bitcast.32, f32[32,128]{1,0:T(8,128)} %bitcast.33, s32[16,128]{1,0:T(8,128)} %bitcast.34, s32[16,128]{1,0:T(8,128)} %bitcast.35, f32[1,144]{1,0:T(1,128)} %bitcast.37), custom_call_target="tpu_custom_call" | custom-call | tf_op jit(solution)/shard_map/schur_step/pallas_call | solution.py:595
  35.4 0.6 %copy.16 = f32[144]{0:T(256)} copy(f32[144]{0:T(256)S(1)} %bitcast.30) | data formatting | bytes 1152
  36.0 0.6 %copy.17 = f32[4,3,128]{2,0,1:T(4,128)} copy(f32[4,3,128]{2,0,1:T(4,128)S(1)} %bitcast.29) | data formatting | bytes 12288

commit v3 on v2

--- a/solution.py
+++ b/solution.py
@@ -96,8 +96,8 @@
         cam_ref, land_ref,
         pairs_ref, cj_ref, lj_ref, re_ref, oc_ref, ol_ref, damp_ref, s0,
         one_cam, one_land, ustat, wstat, xstat, bstat, res, vecs, fac, yvec,
-        msg1, msg2, sums, in1, in2, zbuf, tbuf, own, stot,
-        s1, r1, s2, r2, s3, r3, s4, r4, s5, r5,
+        msg1, msg2, in1, zbuf, in2, in3, hsum, qbuf, own, stot,
+        s1, r1, s2, r2, s3, r3, s4, r4, s5, r5, s6, r6,
     ):
         one = jnp.asarray(1, jnp.bfloat16)
         nil = jnp.asarray(0, jnp.bfloat16)
@@ -433,15 +433,16 @@
         @pl.when(is_hub)
         def _():
             total = at_hub(msg1, in1, s1, r1)
-            sums[...] = total
             zbuf[0, 0:8, :] = total[0:8] / total[8:16]
             zbuf[0, 8:9, :] = total[16:17] / total[17:18]
+            zbuf[0, 9:17, :] = total[8:16]
+            zbuf[0, 17:18, :] = total[17:18]
             spread(zbuf, s2, r2)
             zbuf[1 + row - 2 * col] = zbuf[0]
 
         arrived(zbuf, s2, r2)
 
-        z_tiles = tuple(zbuf[i] for i in range(3))
+        z_tiles = tuple(zbuf[i, 0:9, :] for i in range(3))
         m0, m1, b, y = pushed(z_tiles)
         for i in range(3):
             yvec[3 + i] = y[i]
@@ -467,29 +468,109 @@
                 high = high + damp[8:9] * z_tiles[0][8:9]
             msg2[i, 0:8, :] = low
             msg2[i, 8:9, :] = high
-        to_hubs(msg2, in2, s3, r3)
-        own[...] = jnp.zeros_like(own)
+        mine_tile = 1 + row - 2 * col
+
+        def ring_copy():
+            slot = lax.rem(col - hub_col + n_col, n_col)
+            return pltpu.make_async_remote_copy(
+                src_ref=msg2.at[0],
+                dst_ref=in2.at[slot],
+                send_sem=s3.at[0],
+                recv_sem=r3.at[slot],
+                device_id=(row, hub_col),
+                device_id_type=MESH,
+            )
+
+        def plane_copy(i):
+            return pltpu.make_async_remote_copy(
+                src_ref=msg2.at[pl.ds(1, 2)],
+                dst_ref=in3.at[i],
+                send_sem=s3.at[i],
+                recv_sem=r4.at[i],
+                device_id=(up(i), col),
+                device_id_type=MESH,
+            )
+
+        def rows_copy(i):
+            return pltpu.make_async_remote_copy(
+                src_ref=hsum.at[0],
+                dst_ref=qbuf.at[mine_tile],
+                send_sem=s4.at[i],
+                recv_sem=r6.at[mine_tile],
+                device_id=(up(i), col),
+                device_id_type=MESH,
+            )
+
+        def total_row_copy(i):
+            return pltpu.make_async_remote_copy(
+                src_ref=hsum.at[1],
+                dst_ref=qbuf.at[0],
+                send_sem=s6.at[i],
+                recv_sem=r6.at[0],
+                device_id=(row, over(i)),
+                device_id_type=MESH,
+            )
+
+        @pl.when(jnp.logical_not(is_hub))
+        def _():
+            ring_copy().start()
+
+        for i in plane:
+            plane_copy(i).start()
 
         @pl.when(is_hub)
         def _():
-            q0 = at_hub(msg2, in2, s3, r3)
-            total = sums[...]
-            d_low, d_high = total[8:16], total[17:18]
-            z_low, z_high = zbuf[0, 0:8, :], zbuf[0, 8:9, :]
-            t_low = q0[0:8] / d_low - z_low
-            t_high = q0[8:9] / d_high - z_high
-            tbuf[0, 0:8, :] = t_low
-            tbuf[0, 8:9, :] = t_high
-            spread(tbuf, s4, r4)
-            tbuf[1 + row - 2 * col] = tbuf[0]
-            r_low, r_high = total[0:8], total[16:17]
-            own[0:1, :] = col_sum(r_low * z_low) + r_high * z_high
-            own[1:2, :] = col_sum(r_low * t_low) + r_high * t_high
-            own[2:3, :] = col_sum(t_low * d_low * t_low) + t_high * d_high * t_high
-
-        arrived(tbuf, s4, r4)
-
-        t_tiles = tuple(tbuf[i] for i in range(3))
+            total = msg2[0]
+            for i in ring:
+                pltpu.make_async_remote_copy(
+                    src_ref=msg2.at[0],
+                    dst_ref=in2.at[i],
+                    send_sem=s3.at[0],
+                    recv_sem=r3.at[i],
+                    device_id=(row, over(1)),
+                    device_id_type=MESH,
+                ).wait_recv()
+            for i in ring:
+                total = total + in2[i]
+            hsum[0] = total
+            for i in plane:
+                rows_copy(i).start()
+            qbuf[mine_tile] = total
+
+        for i in plane[::-1]:
+            plane_copy(i).wait_recv()
+        q1, q2 = msg2[1], msg2[2]
+        for i in plane[::-1]:
+            q1 = q1 + in3[i, 0]
+            q2 = q2 + in3[i, 1]
+
+        @pl.when(is_hub)
+        def _():
+            total = hsum[0] + jnp.where(row == 2 * col, q1, q2)
+            hsum[1] = total
+            for i in ring:
+                total_row_copy(i).start()
+            qbuf[0] = total
+
+        for i in range(3):
+            @pl.when(not_self(i))
+            def _():
+                pltpu.make_async_remote_copy(
+                    src_ref=hsum.at[0],
+                    dst_ref=qbuf.at[i],
+                    send_sem=s4.at[1],
+                    recv_sem=r6.at[i],
+                    device_id=(row, over(1)),
+                    device_id_type=MESH,
+                ).wait_recv()
+
+        q_tiles = (qbuf[0], q1 + qbuf[1], q2 + qbuf[2])
+        t_tiles = tuple(q_tiles[i] / zbuf[i, 9:18, :] - z_tiles[i] for i in range(3))
+        at_hub_only = jnp.where(is_hub, zbuf[0, 9:18, :], 0.0)
+        own[0:1, :] = col_sum(at_hub_only * z_tiles[0] * z_tiles[0])
+        own[1:2, :] = col_sum(at_hub_only * z_tiles[0] * t_tiles[0])
+        own[2:3, :] = col_sum(at_hub_only * t_tiles[0] * t_tiles[0])
+
         m0, m1, b, y = pushed(t_tiles)
         for i in range(3):
             yvec[6 + i] = y[i]
@@ -551,9 +632,22 @@
         t_own = jnp.concatenate([chosen(t_tiles[0], 0, 128), chosen(t_tiles[0], 128, 16)], axis=1)
 
         sent_to_hubs(msg1, in1, s1, r1)
-        sent_to_hubs(msg2, in2, s3, r3)
         spread_done(zbuf, s2, r2)
-        spread_done(tbuf, s4, r4)
+
+        @pl.when(jnp.logical_not(is_hub))
+        def _():
+            ring_copy().wait_send()
+
+        for i in plane:
+            plane_copy(i).wait_send()
+
+        @pl.when(is_hub)
+        def _():
+            for i in plane:
+                rows_copy(i).wait_send()
+            for i in ring:
+                total_row_copy(i).wait_send()
+
         total_wait().wait_recv()
         total = jnp.where(quarter == which, col_sum(stot[...]), 0.0)
         scalars = jnp.sum(total, axis=1, keepdims=True)
@@ -573,6 +667,17 @@
         total_wait().wait_send()
 
     return kernel
+
+
+def write_out(cam_ref, land_ref, cam_out, land_out, sem):
+    copies = (
+        pltpu.make_async_copy(cam_ref, cam_out, sem.at[0]),
+        pltpu.make_async_copy(land_ref, land_out, sem.at[1]),
+    )
+    for copy in copies:
+        copy.start()
+    for copy in copies:
+        copy.wait()
 
 
 def per_device(cam_jac, land_jac, resid, obs_cam, obs_land, pairs, cam_damp):
@@ -621,18 +726,20 @@
             pltpu.VMEM((9, 8, LANES), f32),
             pltpu.VMEM((3, 18, LANES), f32),
             pltpu.VMEM((3, 9, LANES), f32),
-            pltpu.VMEM((18, LANES), f32),
             pltpu.VMEM((slots, 18, LANES), f32),
-            pltpu.VMEM((slots, 9, LANES), f32),
-            pltpu.VMEM((3, 9, LANES), f32),
+            pltpu.VMEM((3, 18, LANES), f32),
+            pltpu.VMEM((n_col, 9, LANES), f32),
+            pltpu.VMEM((n_row, 2, 9, LANES), f32),
+            pltpu.VMEM((2, 9, LANES), f32),
             pltpu.VMEM((3, 9, LANES), f32),
             pltpu.VMEM((4, LANES), f32),
             pltpu.VMEM((n_row * n_col, LANES), f32),
             dma((3,)), dma((slots,)),
             dma((slots,)), dma((3,)),
-            dma((3,)), dma((slots,)),
-            dma((slots,)), dma((3,)),
+            dma((n_row,)), dma((n_col,)),
+            dma((n_row,)), dma((n_row,)),
             dma, dma,
+            dma((n_col,)), dma((3,)),
         ],
         compiler_params=pltpu.CompilerParams(collective_id=0, has_side_effects=True, vmem_limit_bytes=VMEM),
         name="schur_step",
@@ -650,6 +757,18 @@
             )
         )
     )
+    cam, land = pl.pallas_call(
+        write_out,
+        out_shape=(
+            jax.ShapeDtypeStruct((1, shard), f32),
+            jax.ShapeDtypeStruct((3, n_cl, LANES), f32),
+        ),
+        in_specs=[vmem] * 2,
+        out_specs=[pl.BlockSpec(memory_space=pltpu.HBM)] * 2,
+        scratch_shapes=[dma((2,))],
+        compiler_params=pltpu.CompilerParams(vmem_limit_bytes=1 << 20),
+        name="write_out",
+    )(cam, land)
     return cam.reshape(shard), land.transpose(1, 0, 2)
 
 

time: 36.7 us -> 34.8 us (0.948)
  local copies, waits for them, and re-layouts: 1.16 us -> 0 us
  Pallas kernels: 34.8 us -> 34 us
    pallas_call x1, Pallas kernels: 34.8 us -> 33.4 us  [per_device(): pl.pallas_call(make_kernel(n_row, n_col, n_cl, n_obs), out_shape=(jax.Sha...]
    unnamed x2 -> x0, local copies, waits for them, and re-layouts: 1.16 us -> none
    pallas_call x0 -> x1, Pallas kernels: none -> 0.62 us  [per_device(): pl.pallas_call(write_out, out_shape=(jax.ShapeDtypeStruct((1, shard), f32...]
where the time goes in v3:
time: 34.8 us; the launch traced here: 34.6 us
  Pallas kernels  34 us (98%)
  between operations  0.64 us (2%)
    pallas_call x1, Pallas kernels, per_device(): pl.pallas_call(make_kernel(n_row, n_col, n_cl, n_obs), out_shape=(jax.Sha...  33.4 us

profile of v3, /device:TPU:1, one launch (start us, length us, event | category | flops | bytes accessed | tf_op | source)
XLA Modules:
  0.0 34.6 jit_solution(2657930168830402762)
XLA Ops:
  0.6 33.4 %schur_step.1 = (f32[1,144]{1,0:T(1,128)S(1)}, f32[3,4,128]{2,1,0:T(4,128)S(1)}) custom-call(s32[2,4]{1,0:T(2,128)} %bitcast.34, f32[288,128]{1,0:T(8,128)} %bitcast.29, f32[96,128]{1,0:T(8,128)} %bitcast.30, f32[32,128]{1,0:T(8,128)} %bitcast.31, s32[16,128]{1,0:T(8,128)} %bitcast.32, s32[16,128]{1,0:T(8,128)} %bitcast.33, f32[1,144]{1,0:T(1,128)} %bitcast.35), custom_call_target="tpu_custom_call" | custom-call | tf_op jit(solution)/shard_map/schur_step/pallas_call | solution.py:700
  34.0 0.6 %write_out.1 = (f32[1,144]{1,0:T(1,128)}, f32[3,4,128]{2,1,0:T(4,128)}) custom-call(f32[1,144]{1,0:T(1,128)S(1)} %get-tuple-element.6.cam_ref, f32[3,4,128]{2,1,0:T(4,128)S(1)} %get-tuple-element.7.land_ref), custom_call_target="tpu_custom_call" | custom-call | tf_op jit(solution)/shard_map/write_out/pallas_call | solution.py:760

commit v4 on v2

--- a/solution.py
+++ b/solution.py
@@ -96,8 +96,8 @@
         cam_ref, land_ref,
         pairs_ref, cj_ref, lj_ref, re_ref, oc_ref, ol_ref, damp_ref, s0,
         one_cam, one_land, ustat, wstat, xstat, bstat, res, vecs, fac, yvec,
-        msg1, msg2, sums, in1, in2, zbuf, tbuf, own, stot,
-        s1, r1, s2, r2, s3, r3, s4, r4, s5, r5,
+        msg1, msg2, in1, zbuf, in2, in3, in4, in5, qbuf, own, stot,
+        s1, r1, s2, r2, s3, r3, s4, r4, s5, r5, s6, r6, s7, r7,
     ):
         one = jnp.asarray(1, jnp.bfloat16)
         nil = jnp.asarray(0, jnp.bfloat16)
@@ -433,15 +433,16 @@
         @pl.when(is_hub)
         def _():
             total = at_hub(msg1, in1, s1, r1)
-            sums[...] = total
             zbuf[0, 0:8, :] = total[0:8] / total[8:16]
             zbuf[0, 8:9, :] = total[16:17] / total[17:18]
+            zbuf[0, 9:17, :] = total[8:16]
+            zbuf[0, 17:18, :] = total[17:18]
             spread(zbuf, s2, r2)
             zbuf[1 + row - 2 * col] = zbuf[0]
 
         arrived(zbuf, s2, r2)
 
-        z_tiles = tuple(zbuf[i] for i in range(3))
+        z_tiles = tuple(zbuf[i, 0:9, :] for i in range(3))
         m0, m1, b, y = pushed(z_tiles)
         for i in range(3):
             yvec[3 + i] = y[i]
@@ -467,29 +468,89 @@
                 high = high + damp[8:9] * z_tiles[0][8:9]
             msg2[i, 0:8, :] = low
             msg2[i, 8:9, :] = high
-        to_hubs(msg2, in2, s3, r3)
-        own[...] = jnp.zeros_like(own)
+        parity = lax.rem(row, 2)
+
+        def send(source, target_ref, send_sem, recv_sem, device):
+            return pltpu.make_async_remote_copy(
+                src_ref=source,
+                dst_ref=target_ref,
+                send_sem=send_sem,
+                recv_sem=recv_sem,
+                device_id=device,
+                device_id_type=MESH,
+            )
+
+        def ring_copy(i):
+            return send(msg2.at[0], in2.at[i], s3.at[i], r3.at[i], (row, over(i)))
+
+        def plane_copy(i):
+            return send(msg2.at[pl.ds(1, 2)], in3.at[i], s4.at[i], r4.at[i], (up(i), col))
+
+        def row_copy(i):
+            slot = parity * n_col + col
+            return send(msg2.at[0], in4.at[slot], s6.at[i], r6.at[slot], (up(i), hub_col))
+
+        def col_copy(j, i):
+            at = j * n_col + i
+            return send(msg2.at[1 + j], in5.at[row], s7.at[at], r7.at[row], (2 * col + j, over(i)))
+
+        sends = [
+            *[row_copy(i) for i in plane if apart(i) > 2],
+            *[col_copy(j, i) for i in ring[:-2] for j in range(2)],
+            *[row_copy(i) for i in plane if apart(i) <= 2],
+            *[col_copy(j, i) for i in ring[-2:] for j in range(2)],
+            *[plane_copy(i) for i in plane],
+            *[ring_copy(i) for i in ring],
+        ]
+        for copy in sends:
+            copy.start()
+
+        for i in ring:
+            ring_copy(i).wait_recv()
+        q_row = msg2[0]
+        for i in ring:
+            q_row = q_row + in2[i]
+        for i in plane[::-1]:
+            plane_copy(i).wait_recv()
+        q_col = [msg2[1], msg2[2]]
+        for i in plane[::-1]:
+            q_col = [q_col[j] + in3[i, j] for j in range(2)]
+
+        @pl.when(jnp.logical_not(is_hub))
+        def _():
+            for i in range(n_row):
+                send(msg2.at[0], in5.at[i], s7.at[1], r7.at[i], (row, over(1))).wait_recv()
+            total = in5[0]
+            for i in range(1, n_row):
+                total = total + in5[i]
+            qbuf[0] = total
 
         @pl.when(is_hub)
         def _():
-            q0 = at_hub(msg2, in2, s3, r3)
-            total = sums[...]
-            d_low, d_high = total[8:16], total[17:18]
-            z_low, z_high = zbuf[0, 0:8, :], zbuf[0, 8:9, :]
-            t_low = q0[0:8] / d_low - z_low
-            t_high = q0[8:9] / d_high - z_high
-            tbuf[0, 0:8, :] = t_low
-            tbuf[0, 8:9, :] = t_high
-            spread(tbuf, s4, r4)
-            tbuf[1 + row - 2 * col] = tbuf[0]
-            r_low, r_high = total[0:8], total[16:17]
-            own[0:1, :] = col_sum(r_low * z_low) + r_high * z_high
-            own[1:2, :] = col_sum(r_low * t_low) + r_high * t_high
-            own[2:3, :] = col_sum(t_low * d_low * t_low) + t_high * d_high * t_high
-
-        arrived(tbuf, s4, r4)
-
-        t_tiles = tuple(tbuf[i] for i in range(3))
+            qbuf[0] = jnp.where(row == 2 * col, q_col[0], q_col[1])
+
+        for j in range(2):
+            @pl.when(row != 2 * col + j)
+            def _():
+                for i in range(n_col):
+                    at = j * n_col + i
+                    send(msg2.at[0], in4.at[at], s6.at[1], r6.at[at], (row, over(1))).wait_recv()
+                total = in4[j * n_col]
+                for i in range(1, n_col):
+                    total = total + in4[j * n_col + i]
+                qbuf[1 + j] = total
+
+            @pl.when(row == 2 * col + j)
+            def _():
+                qbuf[1 + j] = q_row
+
+        q_tiles = (q_row + qbuf[0], q_col[0] + qbuf[1], q_col[1] + qbuf[2])
+        t_tiles = tuple(q_tiles[i] / zbuf[i, 9:18, :] - z_tiles[i] for i in range(3))
+        at_hub_only = jnp.where(is_hub, zbuf[0, 9:18, :], 0.0)
+        own[0:1, :] = col_sum(at_hub_only * z_tiles[0] * z_tiles[0])
+        own[1:2, :] = col_sum(at_hub_only * z_tiles[0] * t_tiles[0])
+        own[2:3, :] = col_sum(at_hub_only * t_tiles[0] * t_tiles[0])
+
         m0, m1, b, y = pushed(t_tiles)
         for i in range(3):
             yvec[6 + i] = y[i]
@@ -551,9 +612,11 @@
         t_own = jnp.concatenate([chosen(t_tiles[0], 0, 128), chosen(t_tiles[0], 128, 16)], axis=1)
 
         sent_to_hubs(msg1, in1, s1, r1)
-        sent_to_hubs(msg2, in2, s3, r3)
         spread_done(zbuf, s2, r2)
-        spread_done(tbuf, s4, r4)
+
+        for copy in sends:
+            copy.wait_send()
+
         total_wait().wait_recv()
         total = jnp.where(quarter == which, col_sum(stot[...]), 0.0)
         scalars = jnp.sum(total, axis=1, keepdims=True)
@@ -573,6 +636,17 @@
         total_wait().wait_send()
 
     return kernel
+
+
+def write_out(cam_ref, land_ref, cam_out, land_out, sem):
+    copies = (
+        pltpu.make_async_copy(cam_ref, cam_out, sem.at[0]),
+        pltpu.make_async_copy(land_ref, land_out, sem.at[1]),
+    )
+    for copy in copies:
+        copy.start()
+    for copy in copies:
+        copy.wait()
 
 
 def per_device(cam_jac, land_jac, resid, obs_cam, obs_land, pairs, cam_damp):
@@ -621,18 +695,22 @@
             pltpu.VMEM((9, 8, LANES), f32),
             pltpu.VMEM((3, 18, LANES), f32),
             pltpu.VMEM((3, 9, LANES), f32),
-            pltpu.VMEM((18, LANES), f32),
             pltpu.VMEM((slots, 18, LANES), f32),
-            pltpu.VMEM((slots, 9, LANES), f32),
-            pltpu.VMEM((3, 9, LANES), f32),
+            pltpu.VMEM((3, 18, LANES), f32),
+            pltpu.VMEM((n_col, 9, LANES), f32),
+            pltpu.VMEM((n_row, 2, 9, LANES), f32),
+            pltpu.VMEM((2 * n_col, 9, LANES), f32),
+            pltpu.VMEM((n_row, 9, LANES), f32),
             pltpu.VMEM((3, 9, LANES), f32),
             pltpu.VMEM((4, LANES), f32),
             pltpu.VMEM((n_row * n_col, LANES), f32),
             dma((3,)), dma((slots,)),
             dma((slots,)), dma((3,)),
-            dma((3,)), dma((slots,)),
-            dma((slots,)), dma((3,)),
+            dma((n_col,)), dma((n_col,)),
+            dma((n_row,)), dma((n_row,)),
             dma, dma,
+            dma((n_row,)), dma((2 * n_col,)),
+            dma((2 * n_col,)), dma((n_row,)),
         ],
         compiler_params=pltpu.CompilerParams(collective_id=0, has_side_effects=True, vmem_limit_bytes=VMEM),
         name="schur_step",
@@ -650,6 +728,18 @@
             )
         )
     )
+    cam, land = pl.pallas_call(
+        write_out,
+        out_shape=(
+            jax.ShapeDtypeStruct((1, shard), f32),
+            jax.ShapeDtypeStruct((3, n_cl, LANES), f32),
+        ),
+        in_specs=[vmem] * 2,
+        out_specs=[pl.BlockSpec(memory_space=pltpu.HBM)] * 2,
+        scratch_shapes=[dma((2,))],
+        compiler_params=pltpu.CompilerParams(vmem_limit_bytes=1 << 20),
+        name="write_out",
+    )(cam, land)
     return cam.reshape(shard), land.transpose(1, 0, 2)
 
 

time: 36.7 us -> 33.6 us (0.916)
  Pallas kernels: 34.8 us -> 32.8 us
  local copies, waits for them, and re-layouts: 1.16 us -> 0 us
    pallas_call x1, Pallas kernels: 34.8 us -> 32.2 us  [per_device(): pl.pallas_call(make_kernel(n_row, n_col, n_cl, n_obs), out_shape=(jax.Sha...]
    unnamed x2 -> x0, local copies, waits for them, and re-layouts: 1.16 us -> none
    pallas_call x0 -> x1, Pallas kernels: none -> 0.62 us  [per_device(): pl.pallas_call(write_out, out_shape=(jax.ShapeDtypeStruct((1, shard), f32...]
where the time goes in v4:
time: 33.6 us; the launch traced here: 33.4 us
  Pallas kernels  32.8 us (98%)
  between operations  0.64 us (2%)
    pallas_call x1, Pallas kernels, per_device(): pl.pallas_call(make_kernel(n_row, n_col, n_cl, n_obs), out_shape=(jax.Sha...  32.2 us

profile of v4, /device:TPU:1, one launch (start us, length us, event | category | flops | bytes accessed | tf_op | source)
XLA Modules:
  0.0 33.4 jit_solution(4496663748036827615)
XLA Ops:
  0.6 32.2 %schur_step.1 = (f32[1,144]{1,0:T(1,128)S(1)}, f32[3,4,128]{2,1,0:T(4,128)S(1)}) custom-call(s32[2,4]{1,0:T(2,128)} %bitcast.34, f32[288,128]{1,0:T(8,128)} %bitcast.29, f32[96,128]{1,0:T(8,128)} %bitcast.30, f32[32,128]{1,0:T(8,128)} %bitcast.31, s32[16,128]{1,0:T(8,128)} %bitcast.32, s32[16,128]{1,0:T(8,128)} %bitcast.33, f32[1,144]{1,0:T(1,128)} %bitcast.35), custom_call_target="tpu_custom_call" | custom-call | tf_op jit(solution)/shard_map/schur_step/pallas_call | solution.py:669
  32.8 0.6 %write_out.1 = (f32[1,144]{1,0:T(1,128)}, f32[3,4,128]{2,1,0:T(4,128)}) custom-call(f32[1,144]{1,0:T(1,128)S(1)} %get-tuple-element.6.cam_ref, f32[3,4,128]{2,1,0:T(4,128)S(1)} %get-tuple-element.7.land_ref), custom_call_target="tpu_custom_call" | custom-call | tf_op jit(solution)/shard_map/write_out/pallas_call | solution.py:731

commit v5 on v4

--- a/solution.py
+++ b/solution.py
@@ -314,6 +314,16 @@
 
         pl.semaphore_wait(barrier, jnp.where(is_hub, 1, 3))
 
+        def many(ref, send_sem, recv_sem):
+            return pltpu.make_async_remote_copy(
+                src_ref=ref,
+                dst_ref=ref,
+                send_sem=send_sem,
+                recv_sem=recv_sem,
+                device_id=(row, over(1)),
+                device_id_type=MESH,
+            )
+
         hub_of = ((row, hub_col), (2 * col, col), (2 * col + 1, col))
 
         def contribution(msg, buf, send, recv, i):
@@ -324,8 +334,8 @@
             return pltpu.make_async_remote_copy(
                 src_ref=msg.at[i],
                 dst_ref=buf.at[slot],
-                send_sem=send.at[i],
-                recv_sem=recv.at[slot],
+                send_sem=send,
+                recv_sem=recv.at[0 if i == 0 else 1],
                 device_id=hub_of[i],
                 device_id_type=MESH,
             )
@@ -339,25 +349,21 @@
                 def _():
                     contribution(msg, buf, send, recv, i).start()
 
-        def sent_to_hubs(msg, buf, send, recv):
-            for i in range(3):
-                @pl.when(not_self(i))
-                def _():
-                    contribution(msg, buf, send, recv, i).wait_send()
+        def sent_to_hubs(msg, send, recv):
+            @pl.when(is_hub)
+            def _():
+                many(msg.at[pl.ds(0, 1)], send, recv.at[0]).wait_send()
+
+            @pl.when(jnp.logical_not(is_hub))
+            def _():
+                many(msg, send, recv.at[0]).wait_send()
 
         def at_hub(msg, buf, send, recv):
             mine_tile = 1 + row - 2 * col
             total = msg[0] + msg[mine_tile]
             late = [n_col + i for i in plane[::-1]]
-            for slot in [*ring, *late]:
-                pltpu.make_async_remote_copy(
-                    src_ref=msg.at[0],
-                    dst_ref=buf.at[slot],
-                    send_sem=send.at[0],
-                    recv_sem=recv.at[slot],
-                    device_id=(row, over(1)),
-                    device_id_type=MESH,
-                ).wait_recv()
+            many(buf.at[pl.ds(1, n_col - 1)], send, recv.at[0]).wait_recv()
+            many(buf.at[pl.ds(n_col + 1, n_row - 1)], send, recv.at[1]).wait_recv()
             for slot in [*ring, *late]:
                 total = total + buf[slot]
             return total
@@ -371,7 +377,7 @@
             return pltpu.make_async_remote_copy(
                 src_ref=buf.at[0],
                 dst_ref=buf.at[slot],
-                send_sem=send.at[j],
+                send_sem=send,
                 recv_sem=recv.at[slot],
                 device_id=target,
                 device_id_type=MESH,
@@ -383,11 +389,10 @@
             for j in others:
                 spread_copy(buf, send, recv, j).start()
 
-        def spread_done(buf, send, recv):
+        def spread_done(proxy, send, recv):
             @pl.when(is_hub)
             def _():
-                for j in others:
-                    spread_copy(buf, send, recv, j).wait_send()
+                many(proxy.at[pl.ds(0, n_row + n_col - 2)], send, recv.at[0]).wait_send()
 
         def arrived(buf, send, recv):
             for i in range(3):
@@ -396,7 +401,7 @@
                     pltpu.make_async_remote_copy(
                         src_ref=buf.at[0],
                         dst_ref=buf.at[i],
-                        send_sem=send.at[1],
+                        send_sem=send,
                         recv_sem=recv.at[i],
                         device_id=(row, over(1)),
                         device_id_type=MESH,
@@ -481,18 +486,17 @@
             )
 
         def ring_copy(i):
-            return send(msg2.at[0], in2.at[i], s3.at[i], r3.at[i], (row, over(i)))
+            return send(msg2.at[0], in2.at[i], s3, r3, (row, over(i)))
 
         def plane_copy(i):
-            return send(msg2.at[pl.ds(1, 2)], in3.at[i], s4.at[i], r4.at[i], (up(i), col))
+            return send(msg2.at[pl.ds(1, 2)], in3.at[i], s4, r4, (up(i), col))
 
         def row_copy(i):
             slot = parity * n_col + col
-            return send(msg2.at[0], in4.at[slot], s6.at[i], r6.at[slot], (up(i), hub_col))
+            return send(msg2.at[0], in4.at[slot], s6, r6.at[parity], (up(i), hub_col))
 
         def col_copy(j, i):
-            at = j * n_col + i
-            return send(msg2.at[1 + j], in5.at[row], s7.at[at], r7.at[row], (2 * col + j, over(i)))
+            return send(msg2.at[1 + j], in5.at[row], s7, r7, (2 * col + j, over(i)))
 
         sends = [
             *[row_copy(i) for i in plane if apart(i) > 2],
@@ -505,21 +509,18 @@
         for copy in sends:
             copy.start()
 
-        for i in ring:
-            ring_copy(i).wait_recv()
+        many(in2.at[pl.ds(1, n_col - 1)], s3, r3).wait_recv()
         q_row = msg2[0]
         for i in ring:
             q_row = q_row + in2[i]
-        for i in plane[::-1]:
-            plane_copy(i).wait_recv()
+        many(in3.at[pl.ds(1, n_row - 1)], s4, r4).wait_recv()
         q_col = [msg2[1], msg2[2]]
         for i in plane[::-1]:
             q_col = [q_col[j] + in3[i, j] for j in range(2)]
 
         @pl.when(jnp.logical_not(is_hub))
         def _():
-            for i in range(n_row):
-                send(msg2.at[0], in5.at[i], s7.at[1], r7.at[i], (row, over(1))).wait_recv()
+            many(in5, s7, r7).wait_recv()
             total = in5[0]
             for i in range(1, n_row):
                 total = total + in5[i]
@@ -532,9 +533,7 @@
         for j in range(2):
             @pl.when(row != 2 * col + j)
             def _():
-                for i in range(n_col):
-                    at = j * n_col + i
-                    send(msg2.at[0], in4.at[at], s6.at[1], r6.at[at], (row, over(1))).wait_recv()
+                many(in4.at[pl.ds(j * n_col, n_col)], s6, r6.at[j]).wait_recv()
                 total = in4[j * n_col]
                 for i in range(1, n_col):
                     total = total + in4[j * n_col + i]
@@ -611,11 +610,13 @@
         z_own = jnp.concatenate([chosen(z_tiles[0], 0, 128), chosen(z_tiles[0], 128, 16)], axis=1)
         t_own = jnp.concatenate([chosen(t_tiles[0], 0, 128), chosen(t_tiles[0], 128, 16)], axis=1)
 
-        sent_to_hubs(msg1, in1, s1, r1)
-        spread_done(zbuf, s2, r2)
-
-        for copy in sends:
-            copy.wait_send()
+        sent_to_hubs(msg1, s1, r1)
+        spread_done(in1, s2, r2)
+
+        many(in2.at[pl.ds(1, n_col - 1)], s3, r3).wait_send()
+        many(in3.at[pl.ds(1, n_row - 1)], s4, r4).wait_send()
+        many(in5.at[pl.ds(1, n_row - 1)], s6, r7).wait_send()
+        many(in4.at[pl.ds(2, 2 * n_col - 2)], s7, r7).wait_send()
 
         total_wait().wait_recv()
         total = jnp.where(quarter == which, col_sum(stot[...]), 0.0)
@@ -704,13 +705,13 @@
             pltpu.VMEM((3, 9, LANES), f32),
             pltpu.VMEM((4, LANES), f32),
             pltpu.VMEM((n_row * n_col, LANES), f32),
-            dma((3,)), dma((slots,)),
-            dma((slots,)), dma((3,)),
-            dma((n_col,)), dma((n_col,)),
-            dma((n_row,)), dma((n_row,)),
+            dma, dma((2,)),
+            dma, dma((3,)),
             dma, dma,
-            dma((n_row,)), dma((2 * n_col,)),
-            dma((2 * n_col,)), dma((n_row,)),
+            dma, dma,
+            dma, dma,
+            dma, dma((2,)),
+            dma, dma,
         ],
         compiler_params=pltpu.CompilerParams(collective_id=0, has_side_effects=True, vmem_limit_bytes=VMEM),
         name="schur_step",

time: 33.6 us -> 32.3 us (0.961)
  Pallas kernels: 32.8 us -> 31.6 us
    pallas_call x1, Pallas kernels: 32.2 us -> 30.9 us  [per_device(): pl.pallas_call(make_kernel(n_row, n_col, n_cl, n_obs), out_shape=(jax.Sha...]
where the time goes in v5:
time: 32.3 us; the launch traced here: 32.2 us
  Pallas kernels  31.6 us (98%)
  between operations  0.64 us (2%)
    pallas_call x1, Pallas kernels, per_device(): pl.pallas_call(make_kernel(n_row, n_col, n_cl, n_obs), out_shape=(jax.Sha...  30.9 us

profile of v5, /device:TPU:1, one launch (start us, length us, event | category | flops | bytes accessed | tf_op | source)
XLA Modules:
  0.0 32.2 jit_solution(10758500599722692163)
XLA Ops:
  0.6 30.9 %schur_step.1 = (f32[1,144]{1,0:T(1,128)S(1)}, f32[3,4,128]{2,1,0:T(4,128)S(1)}) custom-call(s32[2,4]{1,0:T(2,128)} %bitcast.34, f32[288,128]{1,0:T(8,128)} %bitcast.29, f32[96,128]{1,0:T(8,128)} %bitcast.30, f32[32,128]{1,0:T(8,128)} %bitcast.31, s32[16,128]{1,0:T(8,128)} %bitcast.32, s32[16,128]{1,0:T(8,128)} %bitcast.33, f32[1,144]{1,0:T(1,128)} %bitcast.35), custom_call_target="tpu_custom_call" | custom-call | tf_op jit(solution)/shard_map/schur_step/pallas_call | solution.py:670
  31.6 0.6 %write_out.1 = (f32[1,144]{1,0:T(1,128)}, f32[3,4,128]{2,1,0:T(4,128)}) custom-call(f32[1,144]{1,0:T(1,128)S(1)} %get-tuple-element.6.cam_ref, f32[3,4,128]{2,1,0:T(4,128)S(1)} %get-tuple-element.7.land_ref), custom_call_target="tpu_custom_call" | custom-call | tf_op jit(solution)/shard_map/write_out/pallas_call | solution.py:732

commit v6 on v5

--- a/solution.py
+++ b/solution.py
@@ -76,12 +76,12 @@
 
 
 def cholesky_three(v):
-    inv_first = 1.0 / jnp.sqrt(v[0])
+    inv_first = lax.rsqrt(v[0])
     low_one = v[1] * inv_first
     low_two = v[2] * inv_first
-    inv_second = 1.0 / jnp.sqrt(v[3] - low_one * low_one)
+    inv_second = lax.rsqrt(v[3] - low_one * low_one)
     low_three = (v[4] - low_two * low_one) * inv_second
-    inv_third = 1.0 / jnp.sqrt(v[5] - low_two * low_two - low_three * low_three)
+    inv_third = lax.rsqrt(v[5] - low_two * low_two - low_three * low_three)
     return inv_first, low_one, low_two, inv_second, low_three, inv_third
 
 
@@ -364,9 +364,11 @@
             late = [n_col + i for i in plane[::-1]]
             many(buf.at[pl.ds(1, n_col - 1)], send, recv.at[0]).wait_recv()
             many(buf.at[pl.ds(n_col + 1, n_row - 1)], send, recv.at[1]).wait_recv()
-            for slot in [*ring, *late]:
-                total = total + buf[slot]
-            return total
+            slots = [*ring, *late]
+            parts = [total, buf[slots[0]], buf[slots[1]], buf[slots[2]]]
+            for n, slot in enumerate(slots[3:]):
+                parts[n % 4] = parts[n % 4] + buf[slot]
+            return (parts[0] + parts[1]) + (parts[2] + parts[3])
 
         def spread_copy(buf, send, recv, j):
             mine_tile = 1 + row - 2 * col
@@ -623,9 +625,10 @@
         scalars = jnp.sum(total, axis=1, keepdims=True)
         rz, e, f, h = (scalars[i : i + 1] for i in range(4))
         pq = rz + e
-        a0 = rz / pq
-        new = a0 * ((rz * f - e * e) / pq)
-        g = e / pq + new / rz
+        per_pq, per_rz = 1.0 / pq, 1.0 / rz
+        a0 = rz * per_pq
+        new = a0 * ((rz * f - e * e) * per_pq)
+        g = e * per_pq + new * per_rz
         curve = g * g * pq - 2.0 * g * a0 * (e + f) + a0 * a0 * h
         a1 = new / curve
         big_a = a0 + a1 * g

time: 32.3 us -> 32.3 us (level)
  no operation moved by 1% of the time
where the time goes in v6:
time: 32.3 us; the launch traced here: 32.2 us
  Pallas kernels  31.6 us (98%)
  between operations  0.64 us (2%)
    pallas_call x1, Pallas kernels, per_device(): pl.pallas_call(make_kernel(n_row, n_col, n_cl, n_obs), out_shape=(jax.Sha...  30.9 us

profile of v6, /device:TPU:1, one launch (start us, length us, event | category | flops | bytes accessed | tf_op | source)
XLA Modules:
  0.0 32.2 jit_solution(15474502825174276909)
XLA Ops:
  0.6 30.9 %schur_step.1 = (f32[1,144]{1,0:T(1,128)S(1)}, f32[3,4,128]{2,1,0:T(4,128)S(1)}) custom-call(s32[2,4]{1,0:T(2,128)} %bitcast.34, f32[288,128]{1,0:T(8,128)} %bitcast.29, f32[96,128]{1,0:T(8,128)} %bitcast.30, f32[32,128]{1,0:T(8,128)} %bitcast.31, s32[16,128]{1,0:T(8,128)} %bitcast.32, s32[16,128]{1,0:T(8,128)} %bitcast.33, f32[1,144]{1,0:T(1,128)} %bitcast.35), custom_call_target="tpu_custom_call" | custom-call | tf_op jit(solution)/shard_map/schur_step/pallas_call | solution.py:673
  31.6 0.6 %write_out.1 = (f32[1,144]{1,0:T(1,128)}, f32[3,4,128]{2,1,0:T(4,128)}) custom-call(f32[1,144]{1,0:T(1,128)S(1)} %get-tuple-element.6.cam_ref, f32[3,4,128]{2,1,0:T(4,128)S(1)} %get-tuple-element.7.land_ref), custom_call_target="tpu_custom_call" | custom-call | tf_op jit(solution)/shard_map/write_out/pallas_call | solution.py:735
